TPU v7x, 32 devices: a whole 2x2x4 slice. The times are simulated.
32 devices in a mesh: dp: 8 (over z, x), seq: 4 (over y, core).
Axes of the slice: x: 2, y: 2, z: 4, core: 2. Of those that a mesh axis runs over, the one named last changes fastest.
Arguments:
- dec_in: bfloat16 [16, 1024, 768], P('dp', 'seq'), may hold values from -6 to 6
- memory: bfloat16 [16, 512, 768], P('dp', 'seq'), may hold values from -6 to 6
- cotangent: bfloat16 [16, 1024, 768], P('dp', 'seq'), may hold values from -6 to 6
- dec_lengths: int32 [16], P('dp'), may hold values from 1 to 1024, as said below
- mem_mask: int32 [16, 512], P('dp', 'seq'), may hold values from 0 to 1, as said below
- bucket_map: int32 [1024], replicated, may hold values from 0 to 31, as said below
- self_weights: bfloat16 [4, 768, 768], P(None, ('dp', 'seq'))
- cross_weights: bfloat16 [4, 768, 768], P(None, ('dp', 'seq'))
- ffn_in: bfloat16 [2, 768, 2048], P(None, ('dp', 'seq')), may hold values from -0.21875 to 0.21875
- ffn_out: bfloat16 [2048, 768], P(('dp', 'seq')), may hold values from -0.1875 to 0.1875
- norm_gains: float32 [3, 768], replicated, may hold values from 0.5 to 1.5
- bias_table: float32 [32, 12], replicated, may hold values from -3 to 3
Outputs:
- layer_out: bfloat16 [16, 1024, 768], P('dp', 'seq')
- dec_grad: float32 [16, 1024, 768], P('dp', 'seq')
- mem_grad: float32 [16, 512, 768], P('dp', 'seq')
- self_grad: float32 [4, 768, 768], P(None, ('dp', 'seq'))
- cross_grad: float32 [4, 768, 768], P(None, ('dp', 'seq'))
- ffn_in_grad: float32 [2, 768, 2048], P(None, ('dp', 'seq'))
- ffn_out_grad: float32 [2048, 768], P(('dp', 'seq'))
- gains_grad: float32 [3, 768], replicated
- table_grad: float32 [32, 12], replicated
- self_rows: float32 [3, 768], P(None, ('dp', 'seq'))
- self_cols: float32 [3, 768], replicated
- cross_rows: float32 [3, 768], P(None, ('dp', 'seq'))
- cross_cols: float32 [3, 768], replicated
- ffn_in_rows: float32 [2, 768], P(None, ('dp', 'seq'))
- ffn_in_cols: float32 [2, 2048], replicated
- ffn_out_rows: float32 [2048], P(('dp', 'seq'))
- ffn_out_cols: float32 [768], replicated
- out_proj_stats: float32 [2, 2, 768], P(None, None, ('dp', 'seq'))
Inputs may be any that keep to these rules, and one draw needn't show every extreme that they name: `dec_lengths`: the non-padding tokens of a slot are a prefix of its 1024 positions; some slot is full. `mem_mask`: the ones of a slot form a prefix of its 512 rows, at least one; some slot has all 512. `bucket_map`: never falls with the distance; 0 at distance 0; every bucket is used.
All inputs are finite; a program needn't handle non-finite values.
Results may differ from a plain program's by a relative error of at most 0.029.
The roundings to bfloat16 on the way count: a program that leaves them out, or rounds other values in their place, can miss the bound.
Values may be sent and summed in bfloat16 or wider, within the bound.
No kernel may reach another device: no remote copies, remote signals or barrier semaphores. Data moves between devices by JAX's collectives and lax.ppermute only.
A program may use at most 256 MiB of HBM per device.

v0:
```python
import jax
import jax.numpy as jnp
from jax import lax
from jax.sharding import PartitionSpec as P

H = 12
DK = 64
LEN = 1024


epsilon = 1e-06
masked_out = -1000000000.0


def rms_norm(inputs, scales):
    return inputs * lax.rsqrt(jnp.mean(inputs * inputs, axis=-1, keepdims=True) + epsilon) * scales


def gated_unit(gate_pre, up_pre):
    return jax.nn.gelu(gate_pre, approximate=True) * up_pre


def project(inputs, matrix):
    return jnp.einsum("sqk,kn->sqn", inputs, matrix, preferred_element_type=jnp.float32)


def project_back(grads_in, matrix):
    return jnp.einsum("sqn,kn->sqk", grads_in, matrix, preferred_element_type=jnp.float32)


def weight_term(inputs, grads_in):
    return jnp.einsum("sqk,sqn->kn", inputs, grads_in, preferred_element_type=jnp.float32)


def split_heads(inputs):
    return inputs.reshape(inputs.shape[0], inputs.shape[1], H, DK)


def bucket_starts(bucket_map, bucket_count):
    edges = jnp.arange(bucket_count + 1, dtype=jnp.int32)
    below = (bucket_map[:, None] < edges[None, :]).astype(jnp.int32)
    return jnp.sum(below, axis=0)


def bucket_hot(distance, starts):
    lower = starts[:-1]
    upper = starts[1:]
    inside = (distance[:, :, None] >= lower[None, None, :]) & (
        distance[:, :, None] < upper[None, None, :]
    )
    return inside.astype(jnp.float32)


def attention_scores(queries, key_rows, extra, allowed):
    raw_scores = jnp.einsum(
        "sqhd,skhd->shqk",
        split_heads(queries),
        split_heads(key_rows),
        preferred_element_type=jnp.float32,
    )
    return jnp.where(allowed, raw_scores + extra, masked_out)


def attend_forward(queries, key_rows, values, extra, allowed):
    scores = attention_scores(queries, key_rows, extra, allowed)
    row_max = jnp.max(scores, axis=-1, keepdims=True)
    exponent = jnp.exp(scores - row_max)
    row_total = jnp.sum(exponent, axis=-1, keepdims=True)
    shares = (exponent / row_total).astype(jnp.bfloat16)
    mixed_out = jnp.einsum(
        "shqk,skhd->sqhd", shares, split_heads(values), preferred_element_type=jnp.float32
    )
    return (mixed_out.reshape(queries.shape).astype(jnp.bfloat16), row_max + jnp.log(row_total))


def share_parts(queries, key_rows, values, extra, allowed, log_total, grad_mixed):
    scores = attention_scores(queries, key_rows, extra, allowed)
    shares = jnp.exp(scores - log_total)
    grad_shares = jnp.einsum(
        "sqhd,skhd->shqk",
        split_heads(grad_mixed),
        split_heads(values),
        preferred_element_type=jnp.float32,
    )
    return (shares, grad_shares)


def score_grads(shares, grad_shares, row_inner):
    return (shares * (grad_shares - row_inner)).astype(jnp.bfloat16)


def query_side(grad_scores, key_rows, query_shape):
    grad_query = jnp.einsum(
        "shqk,skhd->sqhd", grad_scores, split_heads(key_rows), preferred_element_type=jnp.float32
    )
    return grad_query.reshape(query_shape).astype(jnp.bfloat16)


def key_side(queries, grad_mixed, shares, grad_scores, key_shape):
    grad_keys = jnp.einsum(
        "shqk,sqhd->skhd", grad_scores, split_heads(queries), preferred_element_type=jnp.float32
    )
    grad_values = jnp.einsum(
        "shqk,sqhd->skhd",
        shares.astype(jnp.bfloat16),
        split_heads(grad_mixed),
        preferred_element_type=jnp.float32,
    )
    return (grad_keys.reshape(key_shape), grad_values.reshape(key_shape))


def per_device(
    dec_in,
    memory,
    cotangent,
    dec_lengths,
    mem_mask,
    bucket_map,
    self_weights,
    cross_weights,
    ffn_in,
    ffn_out,
    norm_gains,
    bias_table,
):
    local_weights = (self_weights, cross_weights, ffn_in, ffn_out)
    self_full, cross_full, gate_full, down_full = (
        lax.all_gather(local_weights[0], ("dp", "seq"), axis=1, tiled=True),
        lax.all_gather(local_weights[1], ("dp", "seq"), axis=1, tiled=True),
        lax.all_gather(local_weights[2], ("dp", "seq"), axis=1, tiled=True),
        lax.all_gather(local_weights[3], ("dp", "seq"), axis=0, tiled=True),
    )
    row_count = dec_in.shape[1]
    query_pos = lax.axis_index("seq") * row_count + jnp.arange(row_count, dtype=jnp.int32)
    key_pos = jnp.arange(LEN, dtype=jnp.int32)
    starts = bucket_starts(bucket_map, bias_table.shape[0])
    distance = jnp.maximum(query_pos[:, None] - key_pos[None, :], 0)
    one_hot = bucket_hot(distance, starts)
    pos_bias = jnp.einsum("qkb,bh->hqk", one_hot, bias_table, precision=lax.Precision.HIGHEST)[None]
    causal = (key_pos[None, None, None, :] <= query_pos[None, None, :, None]) & (
        key_pos[None, None, None, :] < dec_lengths[:, None, None, None]
    )
    residual_in = dec_in.astype(jnp.float32)
    self_normed = rms_norm(residual_in, norm_gains[0]).astype(jnp.bfloat16)
    self_query = project(self_normed, self_full[0]).astype(jnp.bfloat16)
    self_keys = project(self_normed, self_full[1]).astype(jnp.bfloat16)
    self_values = project(self_normed, self_full[2]).astype(jnp.bfloat16)
    keys_whole, values_whole = (
        lax.all_gather(self_keys, "seq", axis=1, tiled=True),
        lax.all_gather(self_values, "seq", axis=1, tiled=True),
    )
    self_mixed, self_total = attend_forward(self_query, keys_whole, values_whole, pos_bias, causal)
    first_sum = residual_in + project(self_mixed, self_full[3])
    cross_normed = rms_norm(first_sum, norm_gains[1]).astype(jnp.bfloat16)
    cross_query = project(cross_normed, cross_full[0]).astype(jnp.bfloat16)
    cross_keys = project(memory, cross_full[1]).astype(jnp.bfloat16)
    cross_values = project(memory, cross_full[2]).astype(jnp.bfloat16)
    memory_flags = mem_mask.astype(jnp.bfloat16)
    keys_memory, values_memory, flags_memory = (
        lax.all_gather(cross_keys, "seq", axis=1, tiled=True),
        lax.all_gather(cross_values, "seq", axis=1, tiled=True),
        lax.all_gather(memory_flags, "seq", axis=1, tiled=True),
    )
    visible = (flags_memory > 0.5)[:, None, None, :]
    cross_mixed, cross_total = attend_forward(cross_query, keys_memory, values_memory, 0.0, visible)
    second_sum = first_sum + project(cross_mixed, cross_full[3])
    ffn_normed = rms_norm(second_sum, norm_gains[2]).astype(jnp.bfloat16)
    gate_pre = project(ffn_normed, gate_full[0])
    up_pre = project(ffn_normed, gate_full[1])
    activated, gated_pull = jax.vjp(gated_unit, gate_pre, up_pre)
    hidden = activated.astype(jnp.bfloat16)
    layer_out = (second_sum + project(hidden, down_full)).astype(jnp.bfloat16)
    self_back, cross_back, gate_back, down_back = (
        lax.all_gather(local_weights[0], ("dp", "seq"), axis=1, tiled=True),
        lax.all_gather(local_weights[1], ("dp", "seq"), axis=1, tiled=True),
        lax.all_gather(local_weights[2], ("dp", "seq"), axis=1, tiled=True),
        lax.all_gather(local_weights[3], ("dp", "seq"), axis=0, tiled=True),
    )
    grad_out = cotangent.astype(jnp.float32)
    grad_branch = grad_out.astype(jnp.bfloat16)
    down_grad = weight_term(hidden, grad_branch)
    grad_hidden = project_back(grad_branch, down_back)
    grad_gate, grad_up = gated_pull(grad_hidden)
    grad_gate = grad_gate.astype(jnp.bfloat16)
    grad_up = grad_up.astype(jnp.bfloat16)
    gate_grad = jnp.stack([weight_term(ffn_normed, grad_gate), weight_term(ffn_normed, grad_up)])
    grad_normed = project_back(grad_gate, gate_back[0]) + project_back(grad_up, gate_back[1])
    _, third_pull = jax.vjp(rms_norm, second_sum, norm_gains[2])
    norm_part, gain_third = third_pull(grad_normed)
    grad_second = grad_out + norm_part
    grad_branch = grad_second.astype(jnp.bfloat16)
    cross_out_grad = weight_term(cross_mixed, grad_branch)
    grad_mixed = project_back(grad_branch, cross_back[3]).astype(jnp.bfloat16)
    cross_shares, cross_share_grads = share_parts(
        cross_query, keys_memory, values_memory, 0.0, visible, cross_total, grad_mixed
    )
    cross_inner = jnp.sum(cross_shares * cross_share_grads, axis=-1, keepdims=True)
    cross_score_grad = score_grads(cross_shares, cross_share_grads, cross_inner)
    cross_query_grad = query_side(cross_score_grad, keys_memory, cross_query.shape)
    cross_key_part, cross_value_part = key_side(
        cross_query, grad_mixed, cross_shares, cross_score_grad, keys_memory.shape
    )
    cross_key_grad, cross_value_grad = (
        lax.psum_scatter(
            cross_key_part.astype(jnp.bfloat16), "seq", scatter_dimension=1, tiled=True
        ).astype(jnp.float32),
        lax.psum_scatter(
            cross_value_part.astype(jnp.bfloat16), "seq", scatter_dimension=1, tiled=True
        ).astype(jnp.float32),
    )
    cross_key_grad = cross_key_grad.astype(jnp.bfloat16)
    cross_value_grad = cross_value_grad.astype(jnp.bfloat16)
    cross_grad = jnp.stack(
        [
            weight_term(cross_normed, cross_query_grad),
            weight_term(memory, cross_key_grad),
            weight_term(memory, cross_value_grad),
            cross_out_grad,
        ]
    )
    mem_grad = project_back(cross_key_grad, cross_back[1]) + project_back(
        cross_value_grad, cross_back[2]
    )
    _, second_pull = jax.vjp(rms_norm, first_sum, norm_gains[1])
    norm_part, gain_second = second_pull(project_back(cross_query_grad, cross_back[0]))
    grad_first = grad_second + norm_part
    grad_branch = grad_first.astype(jnp.bfloat16)
    self_out_grad = weight_term(self_mixed, grad_branch)
    grad_mixed = project_back(grad_branch, self_back[3]).astype(jnp.bfloat16)
    self_shares, self_share_grads = share_parts(
        self_query, keys_whole, values_whole, pos_bias, causal, self_total, grad_mixed
    )
    self_inner = jnp.sum(self_shares * self_share_grads, axis=-1, keepdims=True)
    self_score_grad = score_grads(self_shares, self_share_grads, self_inner)
    self_query_grad = query_side(self_score_grad, keys_whole, self_query.shape)
    table_part = jnp.einsum(
        "shqk,qkb->bh",
        self_score_grad.astype(jnp.float32),
        one_hot,
        precision=lax.Precision.HIGHEST,
    )
    self_key_part, self_value_part = key_side(
        self_query, grad_mixed, self_shares, self_score_grad, keys_whole.shape
    )
    self_key_grad, self_value_grad = (
        lax.psum_scatter(
            self_key_part.astype(jnp.bfloat16), "seq", scatter_dimension=1, tiled=True
        ).astype(jnp.float32),
        lax.psum_scatter(
            self_value_part.astype(jnp.bfloat16), "seq", scatter_dimension=1, tiled=True
        ).astype(jnp.float32),
    )
    self_key_grad = self_key_grad.astype(jnp.bfloat16)
    self_value_grad = self_value_grad.astype(jnp.bfloat16)
    self_grad = jnp.stack(
        [
            weight_term(self_normed, self_query_grad),
            weight_term(self_normed, self_key_grad),
            weight_term(self_normed, self_value_grad),
            self_out_grad,
        ]
    )
    grad_normed = (
        project_back(self_query_grad, self_back[0])
        + project_back(self_key_grad, self_back[1])
        + project_back(self_value_grad, self_back[2])
    )
    _, first_pull = jax.vjp(rms_norm, residual_in, norm_gains[0])
    norm_part, gain_first = first_pull(grad_normed)
    dec_grad = grad_first + norm_part
    self_shard, cross_shard, gate_shard, down_shard = (
        lax.psum_scatter(self_grad, ("dp", "seq"), scatter_dimension=1, tiled=True),
        lax.psum_scatter(cross_grad, ("dp", "seq"), scatter_dimension=1, tiled=True),
        lax.psum_scatter(gate_grad, ("dp", "seq"), scatter_dimension=1, tiled=True),
        lax.psum_scatter(down_grad, ("dp", "seq"), scatter_dimension=0, tiled=True),
    )
    self_square = self_shard * self_shard
    cross_square = cross_shard * cross_shard
    gate_square = gate_shard * gate_shard
    down_square = down_shard * down_shard
    stat_terms = (
        jnp.stack([gain_first, gain_second, gain_third]),
        table_part,
        jnp.sum(self_square, axis=1) / self_grad.shape[1],
        jnp.sum(cross_square, axis=1) / cross_grad.shape[1],
        jnp.sum(gate_square, axis=1) / gate_grad.shape[1],
        jnp.sum(down_square, axis=0) / down_grad.shape[0],
    )
    gains_grad, table_grad, self_cols, cross_cols, gate_cols, down_cols = lax.psum(
        (stat_terms[0], stat_terms[1], stat_terms[2], stat_terms[3], stat_terms[4], stat_terms[5]),
        ("dp", "seq"),
    )
    self_row_means = jnp.mean(self_square, axis=2)
    cross_row_means = jnp.mean(cross_square, axis=2)
    shard_rows = self_shard.shape[1]
    column_start = lax.axis_index(("dp", "seq")) * shard_rows
    self_col_piece = lax.dynamic_slice_in_dim(self_cols[3], column_start, shard_rows, 0)
    cross_col_piece = lax.dynamic_slice_in_dim(cross_cols[3], column_start, shard_rows, 0)
    out_proj_stats = jnp.stack(
        [
            jnp.stack([self_row_means[3], self_col_piece]),
            jnp.stack([cross_row_means[3], cross_col_piece]),
        ]
    )
    return (
        layer_out,
        dec_grad,
        mem_grad,
        self_shard,
        cross_shard,
        gate_shard,
        down_shard,
        gains_grad,
        table_grad,
        self_row_means[:3],
        self_cols[:3],
        cross_row_means[:3],
        cross_cols[:3],
        jnp.mean(gate_square, axis=2),
        gate_cols,
        jnp.mean(down_square, axis=1),
        down_cols,
        out_proj_stats,
    )


def solution(mesh):
    in_specs = (
        P("dp", "seq", None),
        P("dp", "seq", None),
        P("dp", "seq", None),
        P("dp"),
        P("dp", "seq"),
        P(),
        P(None, ("dp", "seq"), None),
        P(None, ("dp", "seq"), None),
        P(None, ("dp", "seq"), None),
        P(("dp", "seq"), None),
        P(),
        P(),
    )
    out_specs = (
        P("dp", "seq", None),
        P("dp", "seq", None),
        P("dp", "seq", None),
        P(None, ("dp", "seq"), None),
        P(None, ("dp", "seq"), None),
        P(None, ("dp", "seq"), None),
        P(("dp", "seq"), None),
        P(),
        P(),
        P(None, ("dp", "seq")),
        P(),
        P(None, ("dp", "seq")),
        P(),
        P(None, ("dp", "seq")),
        P(),
        P(("dp", "seq")),
        P(),
        P(None, None, ("dp", "seq")),
    )
    return jax.shard_map(
        per_device, mesh=mesh, in_specs=in_specs, out_specs=out_specs, check_vma=False
    )
```

profile of v0, /device:TPU:0, one launch (start us, length us, event | category | flops | bytes accessed | tf_op | source)
XLA Modules:
  0.0 1453.2 jit_solution(13687406730126101037)
XLA Ops:
  8.8 68.5 %all-gather.15.cloned.1.call-done = bf16[4,768,768]{2,1,0:T(8,128)(2,1)} async-done(((bf16[4,24,768]{2,1,0:T(8,128)(2,1)}), bf16[4,768,768]{2,1,0:T(8,128)(2,1)}) %all-gather.15.cloned.1.call-update) | async-done | bytes 4718608 | tf_op jit(solution)/shard_map/all_gather | solution.py:129
  77.3 2.5 convolution_convert_fusion.10
  79.9 2.5 convolution_convert_fusion.11
  82.8 59.9 %all-gather.9.cloned.1.call-done = bf16[4,768,768]{2,1,0:T(8,128)(2,1)} async-done(((bf16[4,24,768]{2,1,0:T(8,128)(2,1)}), bf16[4,768,768]{2,1,0:T(8,128)(2,1)}) %all-gather.9.cloned.1.call-update) | async-done | bytes 4718608 | tf_op jit(solution)/shard_map/all_gather | solution.py:128
  142.6 3.0 convolution_convert_fusion.5
  145.7 3.0 convolution_convert_fusion.7
  150.9 5.0 all_gather.36
  156.4 7.1 compare_and_fusion
  163.6 370.6 %copy.133 = pred[256,1024,32]{1,2,0:T(32,128)(4,1)S(1)} copy(pred[256,1024,32]{0,2,1:T(32,128)(4,1)S(1)} %compare_and_fusion) | data formatting | bytes 16777216 | tf_op jit(solution)/shard_map/and | solution.py:48
  534.2 14.8 %convolution_bitcast_fusion = f32[12,256,1024]{2,0,1:T(8,128)} fusion(pred[256,1024,32]{1,2,0:T(32,128)(4,1)S(1)} %copy.133, f32[32,12]{0,1:T(8,128)S(1)} %copy-done.66), kind=kOutput, calls=%fused_computation.23 | convolution fusion | flops 1207959552 | bytes 20973056 | tf_op jit(solution)/shard_map/qkb,bh->hqk/dot_general | solution.py:139
  549.0 17.6 %copy.134 = f32[12,256,1024]{2,1,0:T(8,128)} copy(f32[12,256,1024]{2,0,1:T(8,128)} %convolution_bitcast_fusion) | data formatting | bytes 25165824 | tf_op jit(solution)/shard_map/qkb,bh->hqk/dot_general | solution.py:139
  570.9 2.6 copy.138
  573.5 2.6 copy.136
  576.1 3.2 copy.132
  579.3 15.6 %fusion.70 = (f32[2,12,256]{2,1,0:T(8,128)}, f32[2,12,256,1024]{3,2,1,0:T(8,128)}) fusion(f32[12,256,1024]{2,1,0:T(8,128)} %copy.134, bf16[2,256,12,64]{1,3,2,0:T(8,128)(2,1)} %bitcast.228, bf16[2,1024,12,64]{1,3,2,0:T(8,128)(2,1)S(1)} %bitcast.220, pred[2,256,1024]{2,1,0:T(8,128)(4,1)} %broadcast_and_fusion), kind=kOutput, calls=%fused_computation.174 | convolution fusion | flops 824174592 | bytes 42229760 | tf_op jit(solution)/shard_map/sqhd,skhd->shqk/dot_general | solution.py:55
  594.9 11.6 fusion
  606.5 3.2 copy.129
  609.7 11.6 fusion.48
  621.3 2.5 multiply_reduce_fusion.7
  624.4 3.5 convolution_convert_fusion.4
  627.9 2.3 copy.137
  630.2 3.1 select_reduce_fusion
  633.3 3.3 fusion.6
  638.0 4.8 fusion.47
  647.7 6.0 fusion.28
  653.7 3.9 fusion.26
  657.7 9.3 multiply_convert_fusion.2
  667.0 5.2 fusion.25
  672.3 4.7 multiply_reduce_fusion.2
  681.0 7.5 fusion.34
  688.4 5.2 copy.181
  693.6 2.8 copy.184
  696.5 7.8 multiply_reduce_fusion.1
  704.3 6.7 multiply_convert_fusion.1
  713.8 2.9 copy.179
  716.7 3.0 copy.183
  719.7 4.8 convolution_convert_fusion.9
  724.6 3.3 multiply_reduce_fusion.3
  732.8 11.0 fusion.29
  743.8 2.8 copy.145
  748.5 17.9 %multiply_reduce_fusion = (f32[2,12,256]{2,1,0:T(8,128)}, f32[2,12,256,1024]{3,2,1,0:T(8,128)}) fusion(f32[2,12,256,1024]{3,2,1,0:T(8,128)} %get-tuple-element.49, f32[2,12,256]{2,1,0:T(8,128)} %copy-done.51, bf16[2,256,12,64]{1,3,2,0:T(8,128)(2,1)} %bitcast.235, bf16[2,1024,12,64]{1,3,2,0:T(8,128)(2,1)S(1)} %bitcast.226), kind=kOutput, calls=%fused_computation.3 | convolution fusion | flops 824174592 | bytes 54312960 | tf_op jit(solution)/shard_map/sqhd,skhd->shqk/dot_general | solution.py:79
  766.4 22.8 %convert_reduce_fusion = (f32[12,256,1024]{2,1,0:T(8,128)}, bf16[2,12,256,1024]{3,2,1,0:T(8,128)(2,1)S(1)}) fusion(f32[2,12,256,1024]{3,2,1,0:T(8,128)} %get-tuple-element.61, f32[2,12,256]{2,1,0:T(8,128)} %get-tuple-element.60, f32[2,12,256,1024]{3,2,1,0:T(8,128)} %get-tuple-element.49, f32[2,12,256]{2,1,0:T(8,128)} %copy-done.51), kind=kLoop, calls=%fused_computation.1 | loop fusion | flops 34603008 | bytes 75546624 | tf_op jit(solution)/shard_map/shqk,qkb->bh/reduce_sum | solution.py:236
  789.1 5.6 convolution_convert_fusion
  794.8 4.6 copy.144
  801.3 4.7 convolution_bitcast_fusion.1
  807.7 3.5 convolution_bitcast_fusion.4
  811.2 2.3 convolution_bitcast_fusion.7
  819.6 3.9 pad_maximum_fusion.2
  823.5 3.9 convolution_bitcast_fusion.2
  827.4 4.4 convolution_bitcast_fusion.3
  831.9 9.0 pad_maximum_fusion
  842.8 8.6 convolution_convert_fusion.8
  851.4 2.4 convolution_bitcast_fusion.11
  856.0 3.5 convolution_bitcast_fusion.9
  861.7 6.0 pad_maximum_fusion.1
  868.5 16.1 %copy.159 = f32[12,256,1024]{1,0,2:T(8,128)} copy(f32[12,256,1024]{2,1,0:T(8,128)} %get-tuple-element.41) | data formatting | bytes 25165824 | tf_op jit(solution)/shard_map/shqk,qkb->bh/reduce_sum | solution.py:236
  884.6 2.2 fusion.49
  887.1 4.7 add_convert_fusion
  891.8 22.7 %convolution_bitcast_fusion.12 = f32[32,12]{0,1:T(8,128)S(1)} fusion(f32[12,256,1024]{1,0,2:T(8,128)} %copy.159, s32[256,1024]{0,1:T(8,128)S(1)} %copy-done.31, s32[32]{0:T(128)S(1)} %copy-done.74, s32[32]{0:T(128)S(1)} %copy-done.72), kind=kOutput, calls=%fused_computation.117 | convolution fusion | flops 1233125376 | bytes 13633280 | tf_op jit(solution)/shard_map/shqk,qkb->bh/dot_general | solution.py:236
  920.2 37.1 %reduce-scatter.23.cloned.1.call-done = f32[64,768]{1,0:T(8,128)} async-done(((f32[2048,768]{1,0:T(8,128)}), f32[64,768]{1,0:T(8,128)}) %reduce-scatter.23.cloned.1.call-update) | async-done | bytes 196624 | tf_op jit(solution)/shard_map/reduce_scatter | solution.py:275
  958.9 140.7 %reduce-scatter.19.cloned.1.call-done = f32[4,24,768]{2,1,0:T(8,128)} async-done(((f32[4,768,768]{2,1,0:T(8,128)}), f32[4,24,768]{2,1,0:T(8,128)}) %reduce-scatter.19.cloned.1.call-update) | async-done | bytes 294928 | tf_op jit(solution)/shard_map/reduce_scatter | solution.py:273
  1100.7 160.1 %reduce-scatter.21.cloned.1.call-done = f32[2,24,2048]{2,1,0:T(8,128)} async-done(((f32[2,768,2048]{2,1,0:T(8,128)}), f32[2,24,2048]{2,1,0:T(8,128)}) %reduce-scatter.21.cloned.1.call-update) | async-done | bytes 393232 | tf_op jit(solution)/shard_map/reduce_scatter | solution.py:274
  1262.5 140.4 %reduce-scatter.17.cloned.1.call-done = f32[4,24,768]{2,1,0:T(8,128)} async-done(((f32[4,768,768]{2,1,0:T(8,128)}), f32[4,24,768]{2,1,0:T(8,128)}) %reduce-scatter.17.cloned.1.call-update) | async-done | bytes 294928 | tf_op jit(solution)/shard_map/reduce_scatter | solution.py:272
  1404.1 41.3 %all-reduce = (f32[3,768]{1,0:T(4,128)}, f32[32,12]{0,1:T(8,128)}, f32[4,768]{1,0:T(4,128)S(1)}, f32[4,768]{1,0:T(4,128)S(1)}, f32[2,2048]{1,0:T(2,128)}, /*index=5*/f32[768]{0:T(1024)}) all-reduce(f32[3,768]{1,0:T(4,128)S(1)} %pad_maximum_fusion.3, ...), channel_id=1, replica_groups=mesh['dp'=8,'seq'=4] {'dp','seq'}, use_global_device_ids=true, to_apply=%region_24.25 | all-reduce | flops 13696 | bytes 109568 | tf_op jit(solution)/shard_map/psum | solution.py:289
  (288 shorter events, 57.9 us)
Async XLA Ops:
  7.2 70.1 %copy-start = (bf16[2,128,768]{2,1,0:T(8,128)(2,1)S(1)}, bf16[2,128,768]{2,1,0:T(8,128)(2,1)}, u32[]{:S(2)}) copy-start(bf16[2,128,768]{2,1,0:T(8,128)(2,1)} %param.13) | copy-start | bytes 1179652
  7.2 75.2 %copy-start.67 = (f32[3,768]{1,0:T(4,128)S(1)}, f32[3,768]{1,0:T(4,128)}, u32[]{:S(2)}) copy-start(f32[3,768]{1,0:T(4,128)} %param.22) | copy-start | bytes 27652
  7.2 75.3 %copy-start.6 = (bf16[2,256,768]{2,1,0:T(8,128)(2,1)S(1)}, bf16[2,256,768]{2,1,0:T(8,128)(2,1)}, u32[]{:S(2)}) copy-start(bf16[2,256,768]{2,1,0:T(8,128)(2,1)} %param.12) | copy-start | bytes 2359300
  7.2 70.1 %all-gather.15.cloned.1.call-start = ((), (), s32[]{:S(2)}) async-start(), calls=%async_computation.11 | async-start | bytes 4866048 | tf_op jit(solution)/shard_map/all_gather | solution.py:129
  8.0 134.7 %all-gather.9.cloned.1.call-start = ((), (), s32[]{:S(2)}) async-start(), calls=%async_computation.8 | async-start | bytes 4866048 | tf_op jit(solution)/shard_map/all_gather | solution.py:128
  8.7 562.2 %all-gather.19.cloned.1.call-start = ((), (), s32[]{:S(2)}) async-start(), calls=%async_computation.13 | async-start | bytes 1966080 | tf_op jit(solution)/shard_map/all_gather | solution.py:160
  79.8 493.7 %all-gather.17.cloned.1.call-start = ((), (), s32[]{:S(2)}) async-start(), calls=%async_computation.12 | async-start | bytes 1966080 | tf_op jit(solution)/shard_map/all_gather | solution.py:161
  82.4 493.7 %all-gather.13.cloned.1.call-start = ((), (), s32[]{:S(2)}) async-start(), calls=%async_computation.10 | async-start | bytes 3932160 | tf_op jit(solution)/shard_map/all_gather | solution.py:149
  82.5 485.2 %copy-start.53 = (f32[768]{0:T(1024)}, f32[768]{0:T(1024)S(1)}, u32[]{:S(2)}) copy-start(f32[768]{0:T(1024)S(1)} %get-tuple-element.33) | copy-start | bytes 9220
  82.7 66.0 %copy-start.58 = (f32[2,256]{1,0:T(2,128)}, f32[2,256]{1,0:T(2,128)S(1)}, u32[]{:S(2)}) copy-start(f32[2,256]{1,0:T(2,128)S(1)} %fusion.42) | copy-start | bytes 6148
  82.8 484.9 %copy-start.56 = (f32[2,256]{1,0:T(2,128)}, f32[2,256]{1,0:T(2,128)S(1)}, u32[]{:S(2)}) copy-start(f32[2,256]{1,0:T(2,128)S(1)} %fusion.58) | copy-start | bytes 6148
  145.6 5.0 copy-start.81
  145.7 5.0 copy-start.70
  145.7 10.2 copy-start.79
  145.7 460.8 %all-gather.11.cloned.1.call-start = ((), (), s32[]{:S(2)}) async-start(), calls=%async_computation.9 | async-start | bytes 3932160 | tf_op jit(solution)/shard_map/all_gather | solution.py:150
  148.7 499.0 %all-gather.21.cloned.1.call-start = ((), (), s32[]{:S(2)}) async-start(), calls=%async_computation.14 | async-start | bytes 6488064 | tf_op jit(solution)/shard_map/all_gather | solution.py:130
  149.5 508.2 %all-gather.23.cloned.1.call-start = ((), (), s32[]{:S(2)}) async-start(), calls=%async_computation.15 | async-start | bytes 3244032 | tf_op jit(solution)/shard_map/all_gather | solution.py:131
  150.2 663.3 %reduce-scatter.27.cloned.1.call-start = ((), (), s32[]{:S(2)}) async-start(), calls=%async_computation.23 | async-start | bytes 1966080
  150.6 12.9 copy-start.30
  150.9 12.7 copy-start.71
  150.9 12.7 copy-start.73
  163.5 370.6 %copy-start.66 = (f32[32,12]{0,1:T(8,128)S(1)}, f32[32,12]{0,1:T(8,128)}, u32[]{:S(2)}) copy-start(f32[32,12]{0,1:T(8,128)} %param.23) | copy-start | bytes 4612
  579.3 15.6 %copy-start.4 = (bf16[2,1024,768]{1,2,0:T(8,128)(2,1)}, bf16[2,1024,768]{1,2,0:T(8,128)(2,1)S(1)}, u32[]{:S(2)}) copy-start(bf16[2,1024,768]{1,2,0:T(8,128)(2,1)S(1)} %copy.132) | copy-start | bytes 9437188
  609.7 11.6 copy-start.21
  609.7 11.6 copy-start.7
  623.8 104.1 %copy-start.10 = (f32[2,256,768]{2,1,0:T(8,128)}, f32[2,256,768]{2,1,0:T(8,128)S(1)}, u32[]{:S(2)}) copy-start(f32[2,256,768]{2,1,0:T(8,128)S(1)} %get-tuple-element.51) | copy-start | bytes 4718596
  623.8 6.3 copy-start.19
  633.3 4.7 copy-start.1
  633.3 4.7 copy-start.29
  645.9 31.1 %copy-start.12 = (f32[2,256,768]{2,1,0:T(8,128)}, f32[2,256,768]{2,1,0:T(8,128)S(1)}, u32[]{:S(2)}) copy-start(f32[2,256,768]{2,1,0:T(8,128)S(1)} %get-tuple-element.55) | copy-start | bytes 4718596
  647.7 6.0 copy-start.27
  647.7 6.0 copy-start.80
  666.9 5.3 copy-start.42
  667.0 5.3 copy-start.44
  667.0 5.3 copy-start.63
  672.2 4.7 copy-start.61
  672.2 4.7 copy-start.48
  696.4 118.9 %reduce-scatter.25.cloned.1.call-start = ((), (), s32[]{:S(2)}) async-start(), calls=%async_computation.22 | async-start | bytes 1966080
  704.3 6.8 copy-start.26
  719.7 136.3 %reduce-scatter.15.cloned.1.call-start = ((), (), s32[]{:S(2)}) async-start(), calls=%async_computation.17 | async-start | bytes 3932160 | tf_op jit(solution)/shard_map/reduce_scatter | solution.py:249
  732.8 11.0 copy-start.51
  746.6 112.9 %reduce-scatter.13.cloned.1.call-start = ((), (), s32[]{:S(2)}) async-start(), calls=%async_computation.16 | async-start | bytes 3932160 | tf_op jit(solution)/shard_map/reduce_scatter | solution.py:246
  789.1 5.6 copy-start.2
  799.5 157.9 %reduce-scatter.23.cloned.1.call-start = ((), (), s32[]{:S(2)}) async-start(), calls=%async_computation.21 | async-start | bytes 6488064 | tf_op jit(solution)/shard_map/reduce_scatter | solution.py:275
  806.0 5.2 copy-start.11
  806.0 293.6 %reduce-scatter.19.cloned.1.call-start = ((), (), s32[]{:S(2)}) async-start(), calls=%async_computation.19 | async-start | bytes 9732096 | tf_op jit(solution)/shard_map/reduce_scatter | solution.py:273
  823.5 437.4 %reduce-scatter.21.cloned.1.call-start = ((), (), s32[]{:S(2)}) async-start(), calls=%async_computation.20 | async-start | bytes 12976128 | tf_op jit(solution)/shard_map/reduce_scatter | solution.py:274
  823.5 3.9 copy-start.28
  840.9 10.5 copy-start.54
  840.9 10.5 copy-start.57
  841.0 562.0 %reduce-scatter.17.cloned.1.call-start = ((), (), s32[]{:S(2)}) async-start(), calls=%async_computation.18 | async-start | bytes 9732096 | tf_op jit(solution)/shard_map/reduce_scatter | solution.py:272
  842.8 8.6 copy-start.8
  868.5 16.2 %copy-start.37 = (bf16[2,12,64,256]{3,2,1,0:T(8,128)(2,1)S(1)}, bf16[2,12,64,256]{3,2,1,0:T(8,128)(2,1)}, u32[]{:S(2)}) copy-start(bf16[2,12,64,256]{3,2,1,0:T(8,128)(2,1)} %copy-done.36) | copy-start | bytes 2359300
  887.0 4.7 copy-start.31
  887.0 4.7 copy-start.72
  887.0 4.7 copy-start.74
  887.0 27.5 %slice-start = ((s8[4718592]{0:T(1024)(128)(4,1)}), s8[4194304]{0:T(1024)(128)(4,1)S(1)}, s32[]{:S(2)}) async-start(s8[4718592]{0:T(1024)(128)(4,1)} %bitcast.250), calls=%async_computation.24 | async-start | bytes 8388608
  887.0 29.5 %slice-start.2 = ((s8[4718592]{0:T(1024)(128)(4,1)}), s8[4194304]{0:T(1024)(128)(4,1)S(1)}, s32[]{:S(2)}) async-start(s8[4718592]{0:T(1024)(128)(4,1)} %bitcast.256), calls=%async_computation.26 | async-start | bytes 8388608
  891.8 22.8 %copy-start.35 = (bf16[2,128,768]{1,2,0:T(8,128)(2,1)S(1)}, bf16[2,128,768]{1,2,0:T(8,128)(2,1)}, u32[]{:S(2)}) copy-start(bf16[2,128,768]{1,2,0:T(8,128)(2,1)} %copy-done.34) | copy-start | bytes 1179652
  891.8 22.8 %slice-start.1 = ((s8[4718592]{0:T(1024)(128)(4,1)}), s8[524288]{0:T(1024)(128)(4,1)S(1)}, s32[]{:S(2)}) async-start(s8[4718592]{0:T(1024)(128)(4,1)} %bitcast.250), calls=%async_computation.25 | async-start | bytes 1048576
  891.8 23.3 %copy-start.33 = (bf16[2,128,768]{1,2,0:T(8,128)(2,1)S(1)}, bf16[2,128,768]{1,2,0:T(8,128)(2,1)}, u32[]{:S(2)}) copy-start(bf16[2,128,768]{1,2,0:T(8,128)(2,1)} %copy-done.32) | copy-start | bytes 1179652
  891.8 24.8 %slice-start.3 = ((s8[4718592]{0:T(1024)(128)(4,1)}), s8[524288]{0:T(1024)(128)(4,1)S(1)}, s32[]{:S(2)}) async-start(s8[4718592]{0:T(1024)(128)(4,1)} %bitcast.256), calls=%async_computation.27 | async-start | bytes 1048576
  1100.7 345.5 %copy-start.75 = (f32[4,24]{1,0:T(4,128)}, f32[4,24]{1,0:T(4,128)S(1)}, u32[]{:S(2)}) copy-start(f32[4,24]{1,0:T(4,128)S(1)} %broadcast_multiply_fusion.4) | copy-start | bytes 1156
  1404.1 42.2 %copy-start.76 = (f32[4,24]{1,0:T(4,128)}, f32[4,24]{1,0:T(4,128)S(1)}, u32[]{:S(2)}) copy-start(f32[4,24]{1,0:T(4,128)S(1)} %broadcast_multiply_fusion.5) | copy-start | bytes 1156
  (40 other events, 82.4 us)
Sparse Core Ops, SparseCore 0:
  10.9 66.3 all-gather.14
  80.1 62.4 all-gather.8
  144.8 18.4 all-gather.18
  165.3 19.6 all-gather.16
  186.4 28.5 all-gather.12
  216.9 28.5 all-gather.10
  248.4 69.5 all-gather.20
  321.0 57.5 all-gather.22
  696.5 26.9 reduce-scatter.26
  726.1 28.1 reduce-scatter.24
  756.9 37.9 reduce-scatter.14
  799.6 37.1 reduce-scatter.12
  843.0 114.2 reduce-scatter.22
  964.7 134.8 reduce-scatter.18
  1106.1 154.6 reduce-scatter.20
  1268.1 134.7 reduce-scatter.16
where the time goes:
time: 1460 us; the launch traced here: 1450 us
  waiting for transfers between devices  610 us (42%)
  local copies, waits for them, and re-layouts  463 us (32%)
  matrix products  236 us (16%)
  other arithmetic  82.5 us (6%)
  blocking collectives  46.4 us (3%)
  between operations  15.7 us (1%)
    and x1, local copies, waits for them, and re-layouts, bucket_hot(): (distance[:, :, None] >= lower[None, None, :]) & (distance[:, :, None] <...  371 us
    reduce_scatter x1, waiting for transfers between devices, per_device(): lax.psum_scatter(gate_grad, ('dp', 'seq'), scatter_dimension=1, tiled=True)  160 us
    reduce_scatter x1, waiting for transfers between devices, per_device(): lax.psum_scatter(cross_grad, ('dp', 'seq'), scatter_dimension=1, tiled=True)  141 us
    reduce_scatter x1, waiting for transfers between devices, per_device(): lax.psum_scatter(self_grad, ('dp', 'seq'), scatter_dimension=1, tiled=True)  140 us
    all_gather x1, waiting for transfers between devices, per_device(): lax.all_gather(local_weights[1], ('dp', 'seq'), axis=1, tiled=True)  68.5 us
    all_gather x1, waiting for transfers between devices, per_device(): lax.all_gather(local_weights[0], ('dp', 'seq'), axis=1, tiled=True)  59.9 us
    psum x1, blocking collectives, per_device(): lax.psum((stat_terms[0], stat_terms[1], stat_terms[2], stat_terms[3], sta...  41.3 us
    reduce_scatter x1, waiting for transfers between devices, per_device(): lax.psum_scatter(down_grad, ('dp', 'seq'), scatter_dimension=0, tiled=True)  37.1 us
  transfers between devices with their start and end apart: 16, of which 6 were waited for; matrix products, arithmetic and copies ran while one was open for 50% of the time, Pallas kernels for 0%

commit v1 on v0

v1 whole, which is shorter than its diff:
```python
import functools

import jax
import jax.numpy as jnp
from jax import lax
from jax.experimental import pallas as pl
from jax.experimental.pallas import tpu as pltpu
from jax.sharding import PartitionSpec as P

H = 12
DK = 64
PAIR = 2 * DK
WIDE = 4 * DK
EPS = 1e-06
MASKED = -1000000000.0
BF = jnp.bfloat16
F32 = jnp.float32
BUDGET = 60 * 1024 * 1024


def dot_nn(a, b):
    return lax.dot_general(a, b, (((1,), (0,)), ((), ())), preferred_element_type=F32)


def dot_nt(a, b):
    return lax.dot_general(a, b, (((1,), (1,)), ((), ())), preferred_element_type=F32)


def dot_tn(a, b):
    return lax.dot_general(a, b, (((0,), (0,)), ((), ())), preferred_element_type=F32)


def inverse_rms(v):
    return lax.rsqrt(jnp.mean(v * v, axis=-1, keepdims=True) + EPS)


def normed(v, gain):
    return (v * inverse_rms(v) * gain).astype(BF)


def normed_back(v, gain, c):
    r = inverse_rms(v)
    scaled = c * gain
    inner = jnp.mean(v * scaled, axis=-1, keepdims=True)
    dv = r * scaled - v * (r * r * r * inner)
    dgain = jnp.sum(c * v * r, axis=0, keepdims=True)
    return dv, dgain


def shear(rows, sign):
    keys = rows.shape[1]
    r = lax.broadcasted_iota(jnp.int32, (8, 1), 0)
    for bit in (1, 2, 4):
        turned = pltpu.roll(rows, bit if sign > 0 else keys - bit, 1)
        rows = jnp.where((r & bit) != 0, turned, rows)
    return rows


def build_bias(line, off, out_ref):
    count, keys = out_ref.shape
    base = shear(pltpu.roll(jnp.broadcast_to(line, (8, keys)), off + 1, 1), 1)
    for g in range(count // 8):
        out_ref[8 * g : 8 * g + 8, :] = pltpu.roll(base, (8 * g) % keys, 1) if g else base


def sum_diagonals(sum_ref, off):
    count, keys = sum_ref.shape
    total = sum_ref[0:8, :]
    for g in range(1, count // 8):
        total = total + pltpu.roll(sum_ref[8 * g : 8 * g + 8, :], (keys - 8 * g) % keys, 1)
    total = jnp.sum(shear(total, -1), axis=0, keepdims=True)
    return pltpu.roll(jnp.broadcast_to(total, (8, keys)), keys - 1 - off, 1)[0:1]


def low_lanes():
    return lax.broadcasted_iota(jnp.int32, (1, PAIR), 1) < DK


def head_part(x, head):
    low = low_lanes()
    mine = low if head % 2 == 0 else jnp.logical_not(low)
    return jnp.where(mine, x, jnp.zeros_like(x))


def row_limit(start, rows, count, causal):
    if not causal:
        return count
    seen = start + 1 + lax.broadcasted_iota(jnp.int32, (rows, 1), 0)
    return jnp.minimum(seen, count)


def attend(q_ref, k_ref, v_ref, o_ref, lse_ref, bias_ref, s_ref, p_ref, off, counts):
    slots, rows, _ = q_ref.shape
    keys = k_ref.shape[1]
    causal = bias_ref is not None
    cols = lax.broadcasted_iota(jnp.int32, (1, keys), 1)
    low = low_lanes()
    work = [(s, h) for s in range(slots) for h in range(WIDE // DK)]

    def lanes(h):
        return slice((h // 2) * PAIR, (h // 2) * PAIR + PAIR)

    def scores(n):
        s, h = work[n]
        s_ref[n % 2] = dot_nt(head_part(q_ref[s, :, lanes(h)], h), k_ref[s, :, lanes(h)])

    scores(0)
    kept = None
    for n, (s, h) in enumerate(work):
        if n + 1 < len(work):
            scores(n + 1)
        sc = s_ref[n % 2]
        if causal:
            sc = sc + bias_ref[h]
        sc = jnp.where(cols < row_limit(off, rows, counts[s], causal), sc, MASKED)
        top = jnp.max(sc, axis=1, keepdims=True)
        e = jnp.exp(sc - top)
        total = jnp.sum(e, axis=1, keepdims=True)
        p_ref[n % 2] = (e * (1.0 / total)).astype(BF)
        out = dot_nn(p_ref[n % 2], v_ref[s, :, lanes(h)])
        log_total = jnp.broadcast_to(top + jnp.log(total), (rows, PAIR))
        if h % 2 == 0:
            kept = (out, log_total)
        else:
            o_ref[s, :, lanes(h)] = jnp.where(low, kept[0], out).astype(BF)
            lse_ref[s, h // 2] = jnp.where(low, kept[1], log_total)


def attend_back(
    q_ref, k_ref, v_ref, g_ref, lse_ref, dq_ref, dk_ref, dv_ref,
    bias_ref, sum_ref, s_ref, dp_ref, p_ref, ds_ref, off, counts,
):
    slots, rows, _ = q_ref.shape
    keys = k_ref.shape[1]
    causal = bias_ref is not None
    cols = lax.broadcasted_iota(jnp.int32, (1, keys), 1)
    low = low_lanes()
    work = [(s, h) for s in range(slots) for h in range(WIDE // DK)]

    def lanes(h):
        return slice((h // 2) * PAIR, (h // 2) * PAIR + PAIR)

    def products(n):
        s, h = work[n]
        s_ref[n % 2] = dot_nt(head_part(q_ref[s, :, lanes(h)], h), k_ref[s, :, lanes(h)])
        dp_ref[n % 2] = dot_nt(head_part(g_ref[s, :, lanes(h)], h), v_ref[s, :, lanes(h)])

    products(0)
    kept = None
    for n, (s, h) in enumerate(work):
        if n + 1 < len(work):
            products(n + 1)
        sc = s_ref[n % 2]
        if causal:
            sc = sc + bias_ref[h]
        sc = jnp.where(cols < row_limit(off, rows, counts[s], causal), sc, MASKED)
        at = (h % 2) * DK
        p = jnp.exp(sc - lse_ref[s, h // 2, :, at : at + 1])
        dp = dp_ref[n % 2]
        inner = jnp.sum(p * dp, axis=1, keepdims=True)
        ds = (p * (dp - inner)).astype(BF)
        p_ref[n % 2] = p.astype(BF)
        ds_ref[n % 2] = ds
        if causal:
            if s == 0:
                sum_ref[h] = ds.astype(F32)
            else:
                sum_ref[h] += ds.astype(F32)
        ds = ds_ref[n % 2]
        dq = dot_nn(ds, k_ref[s, :, lanes(h)])
        dk = dot_tn(head_part(q_ref[s, :, lanes(h)], h), ds)
        dv = dot_tn(head_part(g_ref[s, :, lanes(h)], h), p_ref[n % 2])
        if h % 2 == 0:
            kept = (dq, dk, dv)
        else:
            dq_ref[s * rows : (s + 1) * rows, lanes(h)] = jnp.where(low, kept[0], dq).astype(BF)
            dk_ref[s * keys : (s + 1) * keys, lanes(h)] = (kept[1] + dk).astype(BF).T
            dv_ref[s * keys : (s + 1) * keys, lanes(h)] = (kept[2] + dv).astype(BF).T


def whole(shape):
    return pl.BlockSpec(shape, lambda b, *_: (0,) * len(shape), pipeline_mode=pl.Buffered(1))


def result(shape):
    return pl.BlockSpec(shape, lambda b, *_: (0,) * len(shape))


def wide(shape):
    return pl.BlockSpec(shape[:-1] + (WIDE,), lambda b, *_: (0,) * (len(shape) - 1) + (b,))


def wide_of(index, shape):
    return pl.BlockSpec((None,) + shape[:-1] + (WIDE,), lambda b, *_: (index,) + (0,) * (len(shape) - 1) + (b,))


def whole_of(index, shape):
    return pl.BlockSpec(
        (None,) + shape, lambda b, *_: (index,) + (0,) * len(shape), pipeline_mode=pl.Buffered(1)
    )


def params():
    return pltpu.CompilerParams(dimension_semantics=("arbitrary",), vmem_limit_bytes=BUDGET)


def self_forward_body(
    lims, x_ref, gain_ref, wq_ref, wk_ref, wv_ref, line_ref,
    q_ref, k_ref, v_ref, o_ref, lse_ref, a_ref, bias_ref, s_ref, p_ref,
):
    slots, keys, width = x_ref.shape
    rows = q_ref.shape[1]
    off = lims[0]

    @pl.when(pl.program_id(0) == 0)
    def _():
        for s in range(slots):
            a_ref[s * keys : (s + 1) * keys, :] = normed(x_ref[s].astype(F32), gain_ref[0:1, :])

    for s in range(slots):
        mine = pl.ds(pl.multiple_of(s * keys + off, 128), rows)
        q_ref[s] = dot_nn(a_ref[mine, :], wq_ref[...]).astype(BF)
        k_ref[s] = dot_nn(a_ref[s * keys : (s + 1) * keys, :], wk_ref[...]).astype(BF)
        v_ref[s] = dot_nn(a_ref[s * keys : (s + 1) * keys, :], wv_ref[...]).astype(BF)
    for h in range(WIDE // DK):
        build_bias(line_ref[0, h : h + 1, :], off, bias_ref.at[h])
    counts = [lims[1 + s] for s in range(slots)]
    attend(q_ref, k_ref, v_ref, o_ref, lse_ref, bias_ref, s_ref, p_ref, off, counts)


def self_forward(lims, x_full, gains, w01, w23, line, rows):
    slots, keys, width = x_full.shape
    blocks = width // WIDE
    return pl.pallas_call(
        self_forward_body,
        grid_spec=pltpu.PrefetchScalarGridSpec(
            num_scalar_prefetch=1,
            grid=(blocks,),
            in_specs=[
                whole((slots, keys, width)),
                whole(gains.shape),
                wide_of(0, (width, width)),
                wide_of(1, (width, width)),
                wide_of(0, (width, width)),
                pl.BlockSpec((1, WIDE // DK, keys), lambda b, *_: (b, 0, 0)),
            ],
            out_specs=[
                wide((slots, rows, width)),
                wide((slots, keys, width)),
                wide((slots, keys, width)),
                wide((slots, rows, width)),
                pl.BlockSpec((slots, 2, rows, PAIR), lambda b, *_: (0, b, 0, 0)),
            ],
            scratch_shapes=[
                pltpu.VMEM((slots * keys, width), BF),
                pltpu.VMEM((WIDE // DK, rows, keys), F32),
                pltpu.VMEM((2, rows, keys), F32),
                pltpu.VMEM((2, rows, keys), BF),
            ],
        ),
        out_shape=[
            jax.ShapeDtypeStruct((slots, rows, width), BF),
            jax.ShapeDtypeStruct((slots, keys, width), BF),
            jax.ShapeDtypeStruct((slots, keys, width), BF),
            jax.ShapeDtypeStruct((slots, rows, width), BF),
            jax.ShapeDtypeStruct((slots, H // 2, rows, PAIR), F32),
        ],
        compiler_params=params(),
        cost_estimate=pl.CostEstimate(
            flops=2 * slots * keys * width * width * 3, bytes_accessed=16 << 20, transcendentals=slots * rows * keys * H
        ),
        name="self_forward",
    )(lims, x_full, gains, w01, w01, w23, line)


def cross_forward_body(
    lims, x_ref, o1_ref, wo_ref, gain_ref, mem_ref, wq_ref, wk_ref, wv_ref,
    h_ref, q_ref, k_ref, v_ref, o_ref, lse_ref, a_ref, s_ref, p_ref,
):
    slots, keys, width = mem_ref.shape
    rows = q_ref.shape[1]

    @pl.when(pl.program_id(0) == 0)
    def _():
        for s in range(slots):
            h = x_ref[s].astype(F32) + dot_nn(o1_ref[s], wo_ref[...])
            h_ref[s] = h
            a_ref[s * rows : (s + 1) * rows, :] = normed(h, gain_ref[1:2, :])

    for s in range(slots):
        q_ref[s] = dot_nn(a_ref[s * rows : (s + 1) * rows, :], wq_ref[...]).astype(BF)
        k_ref[s] = dot_nn(mem_ref[s], wk_ref[...]).astype(BF)
        v_ref[s] = dot_nn(mem_ref[s], wv_ref[...]).astype(BF)
    counts = [lims[1 + s] for s in range(slots)]
    attend(q_ref, k_ref, v_ref, o_ref, lse_ref, None, s_ref, p_ref, 0, counts)


def cross_forward(lims, x, o1, w23, gains, mem_full, c01, c23):
    slots, keys, width = mem_full.shape
    rows = x.shape[1]
    blocks = width // WIDE
    return pl.pallas_call(
        cross_forward_body,
        grid_spec=pltpu.PrefetchScalarGridSpec(
            num_scalar_prefetch=1,
            grid=(blocks,),
            in_specs=[
                whole((slots, rows, width)),
                whole((slots, rows, width)),
                whole_of(1, (width, width)),
                whole(gains.shape),
                whole((slots, keys, width)),
                wide_of(0, (width, width)),
                wide_of(1, (width, width)),
                wide_of(0, (width, width)),
            ],
            out_specs=[
                result((slots, rows, width)),
                wide((slots, rows, width)),
                wide((slots, keys, width)),
                wide((slots, keys, width)),
                wide((slots, rows, width)),
                pl.BlockSpec((slots, 2, rows, PAIR), lambda b, *_: (0, b, 0, 0)),
            ],
            scratch_shapes=[
                pltpu.VMEM((slots * rows, width), BF),
                pltpu.VMEM((2, rows, keys), F32),
                pltpu.VMEM((2, rows, keys), BF),
            ],
        ),
        out_shape=[
            jax.ShapeDtypeStruct((slots, rows, width), F32),
            jax.ShapeDtypeStruct((slots, rows, width), BF),
            jax.ShapeDtypeStruct((slots, keys, width), BF),
            jax.ShapeDtypeStruct((slots, keys, width), BF),
            jax.ShapeDtypeStruct((slots, rows, width), BF),
            jax.ShapeDtypeStruct((slots, H // 2, rows, PAIR), F32),
        ],
        compiler_params=params(),
        cost_estimate=pl.CostEstimate(
            flops=2 * slots * (keys * 2 + rows * 2) * width * width,
            bytes_accessed=14 << 20,
            transcendentals=slots * rows * keys * H,
        ),
        name="cross_forward",
    )(lims, x, o1, w23, gains, mem_full, c01, c01, c23)


def feed_forward_body(
    h1_ref, o2_ref, wo_ref, gain_ref, g_ref, w0_ref, w1_ref, wd_ref,
    out_ref, gh_ref, dgain_ref, dw0_ref, dw1_ref, dwd_ref, h_ref, a_ref, at_ref, acc_ref, da_ref,
):
    step = pl.program_id(0)

    @pl.when(step == 0)
    def _():
        h = h1_ref[...] + dot_nn(o2_ref[...], wo_ref[...])
        h_ref[...] = h
        a = normed(h, gain_ref[2:3, :])
        a_ref[...] = a
        at_ref[...] = a.T
        acc_ref[...] = h
        da_ref[...] = jnp.zeros_like(da_ref)

    a = a_ref[...]
    e = g_ref[...]
    gate = dot_nn(a, w0_ref[...])
    up = dot_nn(a, w1_ref[...])
    c = dot_nt(e, wd_ref[...])
    root = 0.7978845608028654
    square = gate * gate
    th = jnp.tanh(root * gate * (1.0 + 0.044715 * square))
    half = 0.5 * (1.0 + th)
    act = gate * half
    slope = half + 0.5 * gate * (1.0 - th * th) * (root * (1.0 + 3.0 * 0.044715 * square))
    hidden = (act * up).astype(BF)
    dgate = (c * up * slope).astype(BF)
    dup = (c * act).astype(BF)
    acc_ref[...] += dot_nn(hidden, wd_ref[...])
    dwd_ref[...] = dot_tn(hidden, e).astype(BF)
    dw0_ref[...] = dot_nn(at_ref[...], dgate).astype(BF)
    dw1_ref[...] = dot_nn(at_ref[...], dup).astype(BF)
    da_ref[...] += dot_nt(dgate, w0_ref[...]) + dot_nt(dup, w1_ref[...])

    @pl.when(step == pl.num_programs(0) - 1)
    def _():
        out_ref[...] = acc_ref[...].astype(BF)
        dv, dgain = normed_back(h_ref[...], gain_ref[2:3, :], da_ref[...])
        gh_ref[...] = e.astype(F32) + dv
        dgain_ref[...] = dgain


def feed_forward(h1, o2, c23, gains, cot, gate_full, down_full):
    tokens, width = h1.shape
    hidden = down_full.shape[0]
    tile = 512
    return pl.pallas_call(
        feed_forward_body,
        grid_spec=pltpu.PrefetchScalarGridSpec(
            num_scalar_prefetch=0,
            grid=(hidden // tile,),
            in_specs=[
                whole((tokens, width)),
                whole((tokens, width)),
                whole_of(1, (width, width)),
                whole(gains.shape),
                whole((tokens, width)),
                pl.BlockSpec((None, width, tile), lambda b: (0, 0, b)),
                pl.BlockSpec((None, width, tile), lambda b: (1, 0, b)),
                pl.BlockSpec((tile, width), lambda b: (b, 0)),
            ],
            out_specs=[
                result((tokens, width)),
                result((tokens, width)),
                result((1, width)),
                pl.BlockSpec((width, tile), lambda b: (0, b)),
                pl.BlockSpec((width, tile), lambda b: (0, b)),
                pl.BlockSpec((tile, width), lambda b: (b, 0)),
            ],
            scratch_shapes=[
                pltpu.VMEM((tokens, width), F32),
                pltpu.VMEM((tokens, width), BF),
                pltpu.VMEM((width, tokens), BF),
                pltpu.VMEM((tokens, width), F32),
                pltpu.VMEM((tokens, width), F32),
            ],
        ),
        out_shape=[
            jax.ShapeDtypeStruct((tokens, width), BF),
            jax.ShapeDtypeStruct((tokens, width), F32),
            jax.ShapeDtypeStruct((1, width), F32),
            jax.ShapeDtypeStruct((width, hidden), BF),
            jax.ShapeDtypeStruct((width, hidden), BF),
            jax.ShapeDtypeStruct((hidden, width), BF),
        ],
        compiler_params=params(),
        cost_estimate=pl.CostEstimate(
            flops=18 * tokens * hidden * width, bytes_accessed=24 << 20, transcendentals=tokens * hidden
        ),
        name="feed_forward",
    )(h1, o2, c23, gains, cot, gate_full, gate_full, down_full)


def cross_backward_body(
    lims, gh2_ref, h1_ref, o2_ref, wo_ref, gain_ref, mem_ref, q_ref, k_ref, v_ref, lse_ref, wq_ref, wk_ref, wv_ref,
    gh_ref, dgain_ref, dmem_ref, dwq_ref, dwk_ref, dwv_ref, dwo_ref,
    g_ref, at_ref, memt_ref, da_ref, dm_ref, dq_ref, dk_ref, dv_ref, s_ref, dp_ref, p_ref, ds_ref,
):
    step = pl.program_id(0)
    slots, keys, width = mem_ref.shape
    rows = q_ref.shape[1]

    @pl.when(step == 0)
    def _():
        e = gh2_ref[...].astype(BF)
        back = dot_nt(e, wo_ref[...]).astype(BF)
        for b in range(width // WIDE):
            for s in range(slots):
                g_ref[b, s] = back[s * rows : (s + 1) * rows, b * WIDE : (b + 1) * WIDE]
        dwo_ref[...] = dot_tn(o2_ref[...], e).astype(BF)
        at_ref[...] = normed(h1_ref[...], gain_ref[1:2, :]).T
        for s in range(slots):
            memt_ref[:, s * keys : (s + 1) * keys] = mem_ref[s].T
        da_ref[...] = jnp.zeros_like(da_ref)
        dm_ref[...] = jnp.zeros_like(dm_ref)

    counts = [lims[1 + s] for s in range(slots)]
    attend_back(
        q_ref, k_ref, v_ref, g_ref.at[step], lse_ref, dq_ref, dk_ref, dv_ref,
        None, None, s_ref, dp_ref, p_ref, ds_ref, 0, counts,
    )
    dwq_ref[...] = dot_nn(at_ref[...], dq_ref[...]).astype(BF)
    dwk_ref[...] = dot_nn(memt_ref[...], dk_ref[...]).astype(BF)
    dwv_ref[...] = dot_nn(memt_ref[...], dv_ref[...]).astype(BF)
    da_ref[...] += dot_nt(dq_ref[...], wq_ref[...])
    dm_ref[...] += dot_nt(dk_ref[...], wk_ref[...]) + dot_nt(dv_ref[...], wv_ref[...])

    @pl.when(step == pl.num_programs(0) - 1)
    def _():
        dv, dgain = normed_back(h1_ref[...], gain_ref[1:2, :], da_ref[...])
        gh_ref[...] = gh2_ref[...] + dv
        dgain_ref[...] = dgain
        dmem_ref[...] = dm_ref[...].astype(BF)


def cross_backward(lims, gh2, h1, o2, c01, c23, gains, mem_full, q, k, v, lse):
    slots, keys, width = mem_full.shape
    rows = q.shape[1]
    tokens = slots * rows
    blocks = width // WIDE
    square = jax.ShapeDtypeStruct((width, width), BF)
    return pl.pallas_call(
        cross_backward_body,
        grid_spec=pltpu.PrefetchScalarGridSpec(
            num_scalar_prefetch=1,
            grid=(blocks,),
            in_specs=[
                whole((tokens, width)),
                whole((tokens, width)),
                whole((tokens, width)),
                whole_of(1, (width, width)),
                whole(gains.shape),
                whole((slots, keys, width)),
                wide((slots, rows, width)),
                wide((slots, keys, width)),
                wide((slots, keys, width)),
                pl.BlockSpec((slots, 2, rows, PAIR), lambda b, *_: (0, b, 0, 0)),
                wide_of(0, (width, width)),
                wide_of(1, (width, width)),
                wide_of(0, (width, width)),
            ],
            out_specs=[
                result((tokens, width)),
                result((1, width)),
                result((slots * keys, width)),
                wide((width, width)),
                wide((width, width)),
                wide((width, width)),
                result((width, width)),
            ],
            scratch_shapes=[
                pltpu.VMEM((blocks, slots, rows, WIDE), BF),
                pltpu.VMEM((width, tokens), BF),
                pltpu.VMEM((width, slots * keys), BF),
                pltpu.VMEM((tokens, width), F32),
                pltpu.VMEM((slots * keys, width), F32),
                pltpu.VMEM((tokens, WIDE), BF),
                pltpu.VMEM((slots * keys, WIDE), BF),
                pltpu.VMEM((slots * keys, WIDE), BF),
                pltpu.VMEM((2, rows, keys), F32),
                pltpu.VMEM((2, rows, keys), F32),
                pltpu.VMEM((2, rows, keys), BF),
                pltpu.VMEM((2, rows, keys), BF),
            ],
        ),
        out_shape=[
            jax.ShapeDtypeStruct((tokens, width), F32),
            jax.ShapeDtypeStruct((1, width), F32),
            jax.ShapeDtypeStruct((slots * keys, width), BF),
            square,
            square,
            square,
            square,
        ],
        compiler_params=params(),
        cost_estimate=pl.CostEstimate(
            flops=2 * slots * (keys * 4 + rows * 4) * width * width,
            bytes_accessed=20 << 20,
            transcendentals=slots * rows * keys * H,
        ),
        name="cross_backward",
    )(lims, gh2, h1, o2, c23, gains, mem_full, q, k, v, lse, c01, c01, c23)


def self_backward_body(
    lims, gh1_ref, x_ref, o1_ref, wo_ref, gain_ref, line_ref, q_ref, k_ref, v_ref, lse_ref, wq_ref, wk_ref, wv_ref,
    dx_ref, table_ref, dwq_ref, dwk_ref, dwv_ref, dwo_ref,
    g_ref, at_ref, da_ref, dq_ref, dk_ref, dv_ref, bias_ref, sum_ref, s_ref, dp_ref, p_ref, ds_ref,
):
    step = pl.program_id(0)
    slots, keys, width = x_ref.shape
    rows = q_ref.shape[1]
    off = lims[0]

    @pl.when(step == 0)
    def _():
        e = gh1_ref[...].astype(BF)
        back = dot_nt(e, wo_ref[...]).astype(BF)
        for b in range(width // WIDE):
            for s in range(slots):
                g_ref[b, s] = back[s * rows : (s + 1) * rows, b * WIDE : (b + 1) * WIDE]
        dwo_ref[...] = dot_tn(o1_ref[...], e).astype(BF)
        for s in range(slots):
            at_ref[:, s * keys : (s + 1) * keys] = normed(x_ref[s].astype(F32), gain_ref[0:1, :]).T
        da_ref[...] = jnp.zeros_like(da_ref)

    for h in range(WIDE // DK):
        build_bias(line_ref[0, h : h + 1, :], off, bias_ref.at[h])
    counts = [lims[1 + s] for s in range(slots)]
    attend_back(
        q_ref, k_ref, v_ref, g_ref.at[step], lse_ref, dq_ref, dk_ref, dv_ref,
        bias_ref, sum_ref, s_ref, dp_ref, p_ref, ds_ref, off, counts,
    )
    for h in range(WIDE // DK):
        table_ref[0, h : h + 1, :] = sum_diagonals(sum_ref.at[h], off)
    dwq = None
    for s in range(slots):
        mine = pl.ds(pl.multiple_of(s * keys + off, 128), rows)
        dq = dq_ref[s * rows : (s + 1) * rows, :]
        part = dot_nn(at_ref[:, mine], dq)
        dwq = part if dwq is None else dwq + part
        da_ref[mine, :] += dot_nt(dq, wq_ref[...])
    dwq_ref[...] = dwq.astype(BF)
    dwk_ref[...] = dot_nn(at_ref[...], dk_ref[...]).astype(BF)
    dwv_ref[...] = dot_nn(at_ref[...], dv_ref[...]).astype(BF)
    da_ref[...] += dot_nt(dk_ref[...], wk_ref[...]) + dot_nt(dv_ref[...], wv_ref[...])

    @pl.when(step == pl.num_programs(0) - 1)
    def _():
        dx_ref[...] = da_ref[...].astype(BF)


def self_backward(lims, gh1, x_full, o1, w01, w23, gains, line, q, k, v, lse):
    slots, keys, width = x_full.shape
    rows = q.shape[1]
    tokens = slots * rows
    blocks = width // WIDE
    square = jax.ShapeDtypeStruct((width, width), BF)
    heads = WIDE // DK
    return pl.pallas_call(
        self_backward_body,
        grid_spec=pltpu.PrefetchScalarGridSpec(
            num_scalar_prefetch=1,
            grid=(blocks,),
            in_specs=[
                whole((tokens, width)),
                whole((slots, keys, width)),
                whole((tokens, width)),
                whole_of(1, (width, width)),
                whole(gains.shape),
                pl.BlockSpec((1, heads, keys), lambda b, *_: (b, 0, 0)),
                wide((slots, rows, width)),
                wide((slots, keys, width)),
                wide((slots, keys, width)),
                pl.BlockSpec((slots, 2, rows, PAIR), lambda b, *_: (0, b, 0, 0)),
                wide_of(0, (width, width)),
                wide_of(1, (width, width)),
                wide_of(0, (width, width)),
            ],
            out_specs=[
                result((slots * keys, width)),
                pl.BlockSpec((1, heads, keys), lambda b, *_: (b, 0, 0)),
                wide((width, width)),
                wide((width, width)),
                wide((width, width)),
                result((width, width)),
            ],
            scratch_shapes=[
                pltpu.VMEM((blocks, slots, rows, WIDE), BF),
                pltpu.VMEM((width, slots * keys), BF),
                pltpu.VMEM((slots * keys, width), F32),
                pltpu.VMEM((tokens, WIDE), BF),
                pltpu.VMEM((slots * keys, WIDE), BF),
                pltpu.VMEM((slots * keys, WIDE), BF),
                pltpu.VMEM((heads, rows, keys), F32),
                pltpu.VMEM((heads, rows, keys), F32),
                pltpu.VMEM((2, rows, keys), F32),
                pltpu.VMEM((2, rows, keys), F32),
                pltpu.VMEM((2, rows, keys), BF),
                pltpu.VMEM((2, rows, keys), BF),
            ],
        ),
        out_shape=[
            jax.ShapeDtypeStruct((slots * keys, width), BF),
            jax.ShapeDtypeStruct((blocks, heads, keys), F32),
            square,
            square,
            square,
            square,
        ],
        compiler_params=params(),
        cost_estimate=pl.CostEstimate(
            flops=2 * slots * (keys * 4 + rows * 4) * width * width,
            bytes_accessed=30 << 20,
            transcendentals=slots * rows * keys * H,
        ),
        name="self_backward",
    )(lims, gh1, x_full, o1, w23, gains, line, q, k, v, lse, w01, w01, w23)


class Cube:
    def __init__(self, mesh):
        self.sizes = {name: mesh.shape[name] for name in ("dp", "seq")}
        self.bits = {}
        for name, size in self.sizes.items():
            count = size.bit_length() - 1
            assert size == 1 << count
            self.bits[name] = [(name, b) for b in reversed(range(count))]
        self.all = self.bits["dp"] + self.bits["seq"]

    def partner(self, x, dim):
        name, b = dim
        return lax.ppermute(x, name, [(i, i ^ (1 << b)) for i in range(self.sizes[name])])

    def second(self, dim):
        name, b = dim
        return (lax.axis_index(name) >> b) & 1

    def gather(self, x, axis, dims, order):
        lead, tail = x.shape[:axis], x.shape[axis + 1 :]
        x = x.reshape(lead + (1,) * len(dims) + x.shape[axis:])
        for dim in order:
            at = axis + dims.index(dim)
            other = self.partner(x, dim)
            second = self.second(dim) == 1
            x = jnp.concatenate([jnp.where(second, other, x), jnp.where(second, x, other)], axis=at)
        return x.reshape(lead + (-1,) + tail)

    def scatter(self, x, axis, dims, order, last=F32):
        lead, tail = x.shape[:axis], x.shape[axis + 1 :]
        count = 1 << len(dims)
        x = x.reshape(lead + (2,) * len(dims) + (x.shape[axis] // count,) + tail)
        for n, dim in enumerate(order):
            at = axis + dims.index(dim)
            second = self.second(dim)
            send = lax.dynamic_slice_in_dim(x, 1 - second, 1, at)
            keep = lax.dynamic_slice_in_dim(x, second, 1, at)
            got = self.partner(send, dim)
            x = keep.astype(F32) + got.astype(F32)
            x = x.astype(last if n == len(order) - 1 else BF)
        return x.reshape(lead + (-1,) + tail)

    def total(self, x, dims):
        for dim in dims:
            x = x + self.partner(x, dim)
        return x


def per_device(
    mesh,
    dec_in,
    memory,
    cotangent,
    dec_lengths,
    mem_mask,
    bucket_map,
    self_weights,
    cross_weights,
    ffn_in,
    ffn_out,
    norm_gains,
    bias_table,
):
    cube = Cube(mesh)
    everyone = cube.all
    near = cube.bits["seq"]
    far = cube.bits["dp"]
    slots, rows, width = dec_in.shape
    tokens = slots * rows
    buckets = bias_table.shape[0]
    core, across, along = near[-1:], near[:-1], far[-1:]
    rest = far[:-1]
    order_a = rest + along + across + core
    order_b = across + rest + along + core

    gate_full = lax.all_gather(ffn_in, ("dp", "seq"), axis=1, tiled=True)
    x_full = cube.gather(dec_in, 1, near, across + core)
    w01 = cube.gather(self_weights[0:2], 1, everyone, order_a)
    w23 = cube.gather(self_weights[2:4], 1, everyone, order_b)
    mem_full = cube.gather(memory, 1, near, across + core)
    seen = cube.total(jnp.sum(mem_mask, axis=1), near)
    c01 = cube.gather(cross_weights[0:2], 1, everyone, order_a)
    c23 = cube.gather(cross_weights[2:4], 1, everyone, order_b)
    down_full = cube.gather(ffn_out, 0, everyone, order_a)

    positions = bucket_map.shape[0]
    hot = (bucket_map[::-1][None, :] == jnp.arange(buckets, dtype=jnp.int32)[:, None]).astype(F32)
    line = jnp.einsum("bh,bm->hm", bias_table, hot, precision=lax.Precision.HIGHEST)
    line = line.reshape(H * DK // WIDE, WIDE // DK, positions)
    start = (lax.axis_index("seq") * rows).astype(jnp.int32)
    lims = jnp.concatenate([start[None], dec_lengths])
    lims_cross = jnp.concatenate([start[None], seen])

    q1, k1, v1, o1, lse1 = self_forward(lims, x_full, norm_gains, w01, w23, line, rows)
    h1, q2, k2, v2, o2, lse2 = cross_forward(lims_cross, dec_in, o1, w23, norm_gains, mem_full, c01, c23)
    flat = (tokens, width)
    h1 = h1.reshape(flat)
    o1 = o1.reshape(flat)
    o2 = o2.reshape(flat)
    layer_out, gh2, gain_third, dw0, dw1, dwd = feed_forward(
        h1, o2, c23, norm_gains, cotangent.reshape(flat), gate_full, down_full
    )
    gate_part = jnp.stack([dw0, dw1])
    gate_shard = lax.psum_scatter(gate_part, ("dp", "seq"), scatter_dimension=1, tiled=True).astype(F32)
    order_c = core + across + along + rest
    order_d = core + along + rest + across
    down_shard = cube.scatter(dwd, 0, everyone, order_c)
    gh1, gain_second, dmem, cq, ck, cv, co = cross_backward(
        lims_cross, gh2, h1, o2, c01, c23, norm_gains, mem_full, q2, k2, v2, lse2
    )
    cross_shard = jnp.concatenate(
        [
            cube.scatter(jnp.stack([cq, ck]), 1, everyone, order_c),
            cube.scatter(jnp.stack([cv, co]), 1, everyone, order_d),
        ]
    )
    mem_grad = cube.scatter(dmem.reshape(mem_full.shape), 1, near, core + across)
    dx, table, sq, sk, sv, so = self_backward(
        lims, gh1, x_full, o1, w01, w23, norm_gains, line, q1, k1, v1, lse1
    )
    self_shard = jnp.concatenate(
        [
            cube.scatter(jnp.stack([sq, sk]), 1, everyone, order_c),
            cube.scatter(jnp.stack([sv, so]), 1, everyone, order_d),
        ]
    )
    c_first = cube.scatter(dx.reshape(x_full.shape), 1, near, core + across)
    dv, gain_first = normed_back(dec_in.astype(F32).reshape(flat), norm_gains[0:1], c_first.reshape(flat))
    dec_grad = (gh1 + dv).reshape(dec_in.shape)
    table_part = jnp.einsum("hm,bm->bh", table.reshape(H, positions), hot, precision=lax.Precision.HIGHEST)

    self_square = self_shard * self_shard
    cross_square = cross_shard * cross_shard
    gate_square = gate_shard * gate_shard
    down_square = down_shard * down_shard
    hidden = ffn_in.shape[2]
    terms = [
        jnp.concatenate([gain_first, gain_second, gain_third]),
        table_part,
        jnp.sum(self_square, axis=1) / width,
        jnp.sum(cross_square, axis=1) / width,
        jnp.sum(gate_square, axis=1) / width,
        jnp.sum(down_square, axis=0) / hidden,
    ]
    packed = jnp.concatenate([t.reshape(-1, 128) for t in terms])
    packed = cube.total(packed, near + far)
    sums = []
    at = 0
    for t in terms:
        count = t.size // 128
        sums.append(packed[at : at + count].reshape(t.shape))
        at += count
    gains_grad, table_grad, self_cols, cross_cols, gate_cols, down_cols = sums
    self_row_means = jnp.mean(self_square, axis=2)
    cross_row_means = jnp.mean(cross_square, axis=2)
    shard_rows = self_shard.shape[1]
    column_start = lax.axis_index(("dp", "seq")) * shard_rows
    self_col_piece = lax.dynamic_slice_in_dim(self_cols[3], column_start, shard_rows, 0)
    cross_col_piece = lax.dynamic_slice_in_dim(cross_cols[3], column_start, shard_rows, 0)
    out_proj_stats = jnp.stack(
        [
            jnp.stack([self_row_means[3], self_col_piece]),
            jnp.stack([cross_row_means[3], cross_col_piece]),
        ]
    )
    return (
        layer_out.reshape(dec_in.shape),
        dec_grad,
        mem_grad,
        self_shard,
        cross_shard,
        gate_shard,
        down_shard,
        gains_grad,
        table_grad,
        self_row_means[:3],
        self_cols[:3],
        cross_row_means[:3],
        cross_cols[:3],
        jnp.mean(gate_square, axis=2),
        gate_cols,
        jnp.mean(down_square, axis=1),
        down_cols,
        out_proj_stats,
    )


def solution(mesh):
    in_specs = (
        P("dp", "seq", None),
        P("dp", "seq", None),
        P("dp", "seq", None),
        P("dp"),
        P("dp", "seq"),
        P(),
        P(None, ("dp", "seq"), None),
        P(None, ("dp", "seq"), None),
        P(None, ("dp", "seq"), None),
        P(("dp", "seq"), None),
        P(),
        P(),
    )
    out_specs = (
        P("dp", "seq", None),
        P("dp", "seq", None),
        P("dp", "seq", None),
        P(None, ("dp", "seq"), None),
        P(None, ("dp", "seq"), None),
        P(None, ("dp", "seq"), None),
        P(("dp", "seq"), None),
        P(),
        P(),
        P(None, ("dp", "seq")),
        P(),
        P(None, ("dp", "seq")),
        P(),
        P(None, ("dp", "seq")),
        P(),
        P(("dp", "seq")),
        P(),
        P(None, None, ("dp", "seq")),
    )
    return jax.shard_map(
        functools.partial(per_device, mesh),
        mesh=mesh,
        in_specs=in_specs,
        out_specs=out_specs,
        check_vma=False,
    )
```

time: 1460 us -> 509 us (0.35)
  waiting for transfers between devices: 610 us -> 189 us
  local copies, waits for them, and re-layouts: 463 us -> 54.7 us
  matrix products: 236 us -> 1.81 us
  Pallas kernels: 0 us -> 137 us
  starting transfers between devices: 0.65 us -> 64.5 us
  blocking collectives: 46.4 us -> 0 us
  other arithmetic: 82.5 us -> 39.8 us
    reduce_scatter x6 -> x0, waiting for transfers between devices: 478 us -> none  [the longest x1 160 us: per_device(): lax.psum_scatter(gate_grad, ('dp', 'seq'), scatter_dimension=1, tiled=True)]
    and x1 -> x0, local copies, waits for them, and re-layouts: 371 us -> none  [bucket_hot(): (distance[:, :, None] >= lower[None, None, :]) & (distance[:, :, None] <...]
    dot_general x47 -> x2, matrix products: 236 us -> 1.81 us  [the longest x1 1.64 us: per_device(): jnp.einsum('hm,bm->bh', table.reshape(H, positions), hot, precision=lax.P...]
    ppermute x0 -> x65, waiting for transfers between devices: none -> 189 us  [partner(): lax.ppermute(x, name, [(i, i ^ 1 << b) for i in range(self.sizes[name])])]
    pallas_call x0 -> x5, Pallas kernels: none -> 137 us  [the longest x1 44.2 us: self_backward(): pl.pallas_call(self_backward_body, grid_spec=pltpu.PrefetchScalarGridSpec...]
    all_gather x8 -> x1, waiting for transfers between devices: 128 us -> 0.01 us  [per_device(): gate_full = lax.all_gather(ffn_in, ('dp', 'seq'), axis=1, tiled=True)]
    ppermute x0 -> x65, starting transfers between devices: none -> 64.4 us  [partner(): lax.ppermute(x, name, [(i, i ^ 1 << b) for i in range(self.sizes[name])])]
    psum x1 -> x0, blocking collectives: 41.3 us -> none  [per_device(): lax.psum((stat_terms[0], stat_terms[1], stat_terms[2], stat_terms[3], sta...]
  transfers between devices with their start and end apart: 16 -> 67, of which waited for: 6 -> 31; matrix products, arithmetic and copies ran while one was open for 50% -> 16% of each run, Pallas kernels for 0% -> 8%
where the time goes in v1:
time: 509 us; the launch traced here: 502 us
  waiting for transfers between devices  189 us (37%)
  Pallas kernels  137 us (27%)
  starting transfers between devices  64.5 us (13%)
  local copies, waits for them, and re-layouts  54.7 us (11%)
  other arithmetic  39.8 us (8%)
  between operations  15.7 us (3%)
    ppermute x65, waiting for transfers between devices, partner(): lax.ppermute(x, name, [(i, i ^ 1 << b) for i in range(self.sizes[name])])  189 us
    ppermute x65, starting transfers between devices, partner(): lax.ppermute(x, name, [(i, i ^ 1 << b) for i in range(self.sizes[name])])  64.4 us
    pallas_call x1, Pallas kernels, self_backward(): pl.pallas_call(self_backward_body, grid_spec=pltpu.PrefetchScalarGridSpec...  44.2 us
    unnamed x64, local copies, waits for them, and re-layouts  28.8 us
    pallas_call x1, Pallas kernels, self_forward(): pl.pallas_call(self_forward_body, grid_spec=pltpu.PrefetchScalarGridSpec(...  26.7 us
    pallas_call x1, Pallas kernels, cross_backward(): pl.pallas_call(cross_backward_body, grid_spec=pltpu.PrefetchScalarGridSpe...  25.7 us
    pallas_call x1, Pallas kernels, feed_forward(): pl.pallas_call(feed_forward_body, grid_spec=pltpu.PrefetchScalarGridSpec(...  24.5 us
    pallas_call x1, Pallas kernels, cross_forward(): pl.pallas_call(cross_forward_body, grid_spec=pltpu.PrefetchScalarGridSpec...  15.5 us
  transfers between devices with their start and end apart: 67, of which 31 were waited for; matrix products, arithmetic and copies ran while one was open for 16% of the time, Pallas kernels for 8%

profile of v1, /device:TPU:0, one launch (start us, length us, event | category | flops | bytes accessed | tf_op | source)
XLA Modules:
  0.0 501.8 jit_solution(17237162402158998993)
XLA Ops:
  7.3 4.1 collective-permute-start.26
  12.4 1.8 collective-permute-start.9
  15.2 2.7 collective-permute-start.16
  29.6 2.6 collective-permute-start.22
  32.3 1.6 collective-permute-start.5
  34.0 11.6 %collective-permute-done.10 = bf16[2,1,1,1,2,1,24,768]{7,6,0,5,4,3,2,1:T(8,128)(2,1)S(1)} collective-permute-done((bf16[2,1,1,1,2,1,24,768]{7,6,0,5,4,3,2,1:T(8,128)(2,1)S(1)}, bf16[2,1,1,1,2,1,24,768]{7,6,0,5,4,3,2,1:T(8,128)(2,1)S(1)}, u32[]{:S(2)}, u32[]{:S(2)}) %collective-permute-start.10) | collective-permute-done | bytes 147488 | tf_op jit(solution)/shard_map/ppermute | solution.py:683
  45.6 2.5 collective-permute-done.22
  48.2 2.1 collective-permute-start.11
  50.4 3.8 collective-permute-done.17
  54.3 8.0 %collective-permute-done.27 = bf16[2,1,1,1,1,64,768]{6,5,4,3,2,1,0:T(8,128)(2,1)S(1)} collective-permute-done((bf16[2,1,1,1,1,64,768]{6,5,4,3,2,1,0:T(8,128)(2,1)S(1)}, bf16[2,1,1,1,1,64,768]{6,5,4,3,2,1,0:T(8,128)(2,1)S(1)}, u32[]{:S(2)}, u32[]{:S(2)}) %collective-permute-start.27) | collective-permute-done | bytes 196640 | tf_op jit(solution)/shard_map/ppermute | solution.py:683
  64.6 6.7 %collective-permute-done.11 = bf16[2,2,1,1,2,1,24,768]{7,6,0,5,4,3,2,1:T(8,128)(2,1)S(1)} collective-permute-done((bf16[2,2,1,1,2,1,24,768]{7,6,0,5,4,3,2,1:T(8,128)(2,1)S(1)}, bf16[2,2,1,1,2,1,24,768]{7,6,0,5,4,3,2,1:T(8,128)(2,1)S(1)}, u32[]{:S(2)}, u32[]{:S(2)}) %collective-permute-start.11) | collective-permute-done | bytes 294944 | tf_op jit(solution)/shard_map/ppermute | solution.py:683
  72.9 3.6 collective-permute-done.23
  79.1 11.1 %collective-permute-done.28 = bf16[2,2,1,1,1,64,768]{6,5,4,3,2,1,0:T(8,128)(2,1)S(1)} collective-permute-done((bf16[2,2,1,1,1,64,768]{6,5,4,3,2,1,0:T(8,128)(2,1)S(1)}, bf16[2,2,1,1,1,64,768]{6,5,4,3,2,1,0:T(8,128)(2,1)S(1)}, u32[]{:S(2)}, u32[]{:S(2)}) %collective-permute-start.28) | collective-permute-done | bytes 393248 | tf_op jit(solution)/shard_map/ppermute | solution.py:683
  92.7 14.6 %collective-permute-done.12 = bf16[2,2,2,1,2,1,24,768]{7,6,0,5,4,3,2,1:T(8,128)(2,1)S(1)} collective-permute-done((bf16[2,2,2,1,2,1,24,768]{7,6,0,5,4,3,2,1:T(8,128)(2,1)S(1)}, bf16[2,2,2,1,2,1,24,768]{7,6,0,5,4,3,2,1:T(8,128)(2,1)S(1)}, u32[]{:S(2)}, u32[]{:S(2)}) %collective-permute-start.12) | collective-permute-done | bytes 589856 | tf_op jit(solution)/shard_map/ppermute | solution.py:683
  108.7 9.5 %collective-permute-done.24 = bf16[2,2,2,1,2,1,24,768]{7,6,0,5,4,3,2,1:T(8,128)(2,1)S(1)} collective-permute-done((bf16[2,2,2,1,2,1,24,768]{7,6,0,5,4,3,2,1:T(8,128)(2,1)S(1)}, bf16[2,2,2,1,2,1,24,768]{7,6,0,5,4,3,2,1:T(8,128)(2,1)S(1)}, u32[]{:S(2)}, u32[]{:S(2)}) %collective-permute-start.24) | collective-permute-done | bytes 589856 | tf_op jit(solution)/shard_map/ppermute | solution.py:683
  121.7 8.5 %collective-permute-done.29 = bf16[2,2,2,1,1,64,768]{6,5,4,3,2,1,0:T(8,128)(2,1)S(1)} collective-permute-done((bf16[2,2,2,1,1,64,768]{6,5,4,3,2,1,0:T(8,128)(2,1)S(1)}, bf16[2,2,2,1,1,64,768]{6,5,4,3,2,1,0:T(8,128)(2,1)S(1)}, u32[]{:S(2)}, u32[]{:S(2)}) %collective-permute-start.29) | collective-permute-done | bytes 786464 | tf_op jit(solution)/shard_map/ppermute | solution.py:683
  133.4 1.6 copy.73
  135.0 1.7 copy.72
  136.7 1.6 copy.70
  138.3 1.7 copy.69
  140.5 2.0 copy.68
  142.4 26.7 %self_forward.1 = (bf16[2,256,768]{2,1,0:T(8,128)(2,1)}, bf16[2,1024,768]{2,1,0:T(8,128)(2,1)}, bf16[2,1024,768]{2,1,0:T(8,128)(2,1)}, bf16[2,256,768]{2,1,0:T(8,128)(2,1)}, f32[2,6,256,128]{3,2,1,0:T(8,128)}) custom-call(s32[3]{0:T(128)} %pad_add_fusion.1.lims, bf16[2,1024,768]{2,1,0:T(8,128)(2,1)} %bitcast.166, f32[3,768]{1,0:T(4,128)} %gain_ref.9, ...), custom_call_target="tpu_custom_call" | custom-call | flops 7247757312 | bytes 16777216 | tf_op jit(solution)/shard_map/self_forward/pallas_call | solution.py:234
  169.1 15.5 %cross_forward.1 = (f32[2,256,768]{2,1,0:T(8,128)}, bf16[2,256,768]{2,1,0:T(8,128)(2,1)}, bf16[2,512,768]{2,1,0:T(8,128)(2,1)}, bf16[2,512,768]{2,1,0:T(8,128)(2...) custom-call(s32[3]{0:T(128)} %pad_add_fusion.lims, bf16[2,256,768]{2,1,0:T(8,128)(2,1)} %x_ref.1, ...), custom_call_target="tpu_custom_call" | custom-call | flops 3623878656 | bytes 14680064 | tf_op jit(solution)/shard_map/cross_forward/pallas_call | solution.py:302
  184.6 1.8 broadcast_select_fusion.1
  186.4 2.0 pad_maximum_fusion.2
  188.4 24.5 %feed_forward.1 = (bf16[512,768]{1,0:T(8,128)(2,1)}, f32[512,768]{1,0:T(8,128)}, f32[1,768]{1,0:T(1,128)}, bf16[768,2048]{1,0:T(8,128)(2,1)}, bf16[768,2048]{1,0:T(8,128)(2,1)}, /*index=5*/bf16[2048,768]{1,0:T(8,128)(2,1)}) custom-call(f32[512,768]{1,0:T(8,128)} %bitcast.201, bf16[512,768]{1,0:T(8,128)(2,1)} %bitcast.205, bf16[2,768,768]{2,1,0:T(8,128)(2,1)} %bitcast.181, ...), custom_call_target="tpu_custom_call" | custom-call | flops 14495514624 | bytes 25165824 | tf_op jit(solution)/shard_map/feed_forward/pallas_call | solution.py:397
  212.9 25.7 %cross_backward.1 = (f32[512,768]{1,0:T(8,128)}, f32[1,768]{1,0:T(1,128)}, bf16[1024,768]{1,0:T(8,128)(2,1)}, bf16[768,768]{1,0:T(8,128)(2,1)}, bf16[768,768]{1,...) custom-call(s32[3]{0:T(128)} %pad_add_fusion.lims, f32[512,768]{1,0:T(8,128)} %get-tuple-element.52.gh2_ref, ...), custom_call_target="tpu_custom_call" | custom-call | flops 7247757312 | bytes 20971520 | tf_op jit(solution)/shard_map/cross_backward/pallas_call | solution.py:492
  238.6 44.2 %self_backward.1 = (bf16[2048,768]{1,0:T(8,128)(2,1)}, f32[3,4,1024]{2,1,0:T(4,128)}, bf16[768,768]{1,0:T(8,128)(2,1)}, bf16[768,768]{1,0:T(8,128)(2,1)}, bf16[7...) custom-call(s32[3]{0:T(128)} %pad_add_fusion.1.lims, f32[512,768]{1,0:T(8,128)} %get-tuple-element.57.gh1_ref, ...), custom_call_target="tpu_custom_call" | custom-call | flops 12079595520 | bytes 31457280 | tf_op jit(solution)/shard_map/self_backward/pallas_call | solution.py:610
  282.8 2.1 constant_dynamic-slice_fusion.26
  293.9 13.0 %copy.89 = bf16[2,768,2048]{2,0,1:T(2,128)(2,1)S(1)} copy(bf16[2,768,2048]{2,1,0:T(8,128)(2,1)S(1)} %pad_maximum_fusion) | data formatting | bytes 12582912
  306.9 6.6 %copy.97 = bf16[96,8,2,2048]{3,1,2,0:T(8,128)(2,1)} copy(bf16[96,8,2,2048]{3,2,1,0:T(2,128)(2,1)S(1)} %bitcast.146) | data formatting | bytes 12582912
  313.6 2.5 fusion.13
  317.8 1.6 fusion.15
  322.6 1.6 add_convert_fusion.7
  324.6 1.7 add_convert_fusion.3
  327.6 1.6 add_convert_fusion.5
  330.9 1.5 collective-permute-start.51
  332.9 5.5 %collective-permute-done.34 = bf16[2,1,1,128,768]{4,3,0,2,1:T(8,128)(2,1)S(1)} collective-permute-done((bf16[2,1,1,128,768]{4,3,0,2,1:T(8,128)(2,1)S(1)}, bf16[2,1,1,128,768]{4,3,0,2,1:T(8,128)(2,1)S(1)}, u32[]{:S(2)}, u32[]{:S(2)}) %collective-permute-start.34) | collective-permute-done | bytes 393248 | tf_op jit(solution)/shard_map/ppermute | solution.py:683
  339.5 2.5 collective-permute-start.41
  342.0 2.1 add_convert_fusion.1
  346.0 1.8 add_convert_fusion
  348.8 2.2 collective-permute-done.46
  351.3 2.6 collective-permute-start.47
  354.1 9.6 %collective-permute-done.36 = bf16[2,2,2,2,1,1,24,768]{7,6,0,5,4,3,2,1:T(8,128)(2,1)S(1)} collective-permute-done((bf16[2,2,2,2,1,1,24,768]{7,6,0,5,4,3,2,1:T(8,128)(2,1)S(1)}, bf16[2,2,2,2,1,1,24,768]{7,6,0,5,4,3,2,1:T(8,128)(2,1)S(1)}, u32[]{:S(2)}, u32[]{:S(2)}) %collective-permute-start.36) | collective-permute-done | bytes 589856 | tf_op jit(solution)/shard_map/ppermute | solution.py:683
  363.7 2.4 collective-permute-start.52
  368.7 31.5 %collective-permute-done.52 = bf16[2,1,2,1,2,1,24,768]{7,6,0,5,4,3,2,1:T(8,128)(2,1)S(1)} collective-permute-done((bf16[2,1,2,1,2,1,24,768]{7,6,0,5,4,3,2,1:T(8,128)(2,1)S(1)}, bf16[2,1,2,1,2,1,24,768]{7,6,0,5,4,3,2,1:T(8,128)(2,1)S(1)}, u32[]{:S(2)}, u32[]{:S(2)}) %collective-permute-start.52) | collective-permute-done | bytes 294944 | tf_op jit(solution)/shard_map/ppermute | solution.py:683
  400.3 5.1 %collective-permute-start.53 = (bf16[2,1,1,1,2,1,24,768]{7,6,0,5,4,3,2,1:T(8,128)(2,1)S(1)}, bf16[2,1,1,1,2,1,24,768]{7,6,0,5,4,3,2,1:T(8,128)(2,1)S(1)}, u32[]{:S(2)}, u32[]{:S(2)}) collective-permute-start(bf16[2,1,1,1,2,1,24,768]{7,6,0,5,4,3,2,1:T(8,128)(2,1)S(1)} %constant_dynamic-slice_fusion.6), channel_id=1, source_target_pairs={{0,8},{4,12},{8,0},{12,4},{16,24},{20,28},{24,16},{28,20},{1,9},{5... | collective-permute-start | bytes 442376 | tf_op jit(solution)/shard_map/ppermute | solution.py:683
  405.5 7.0 %collective-permute-done.42 = bf16[2,1,2,1,2,1,24,768]{7,6,0,5,4,3,2,1:T(8,128)(2,1)S(1)} collective-permute-done((bf16[2,1,2,1,2,1,24,768]{7,6,0,5,4,3,2,1:T(8,128)(2,1)S(1)}, bf16[2,1,2,1,2,1,24,768]{7,6,0,5,4,3,2,1:T(8,128)(2,1)S(1)}, u32[]{:S(2)}, u32[]{:S(2)}) %collective-permute-start.42) | collective-permute-done | bytes 294944 | tf_op jit(solution)/shard_map/ppermute | solution.py:683
  412.6 6.0 %collective-permute-done.48 = bf16[2,1,2,1,1,1,24,768]{7,6,0,5,4,3,2,1:T(8,128)(2,1)S(1)} collective-permute-done((bf16[2,1,2,1,1,1,24,768]{7,6,0,5,4,3,2,1:T(8,128)(2,1)S(1)}, bf16[2,1,2,1,1,1,24,768]{7,6,0,5,4,3,2,1:T(8,128)(2,1)S(1)}, u32[]{:S(2)}, u32[]{:S(2)}) %collective-permute-start.48) | collective-permute-done | bytes 147488 | tf_op jit(solution)/shard_map/ppermute | solution.py:683
  420.9 4.9 collective-permute-done.38
  426.3 6.0 %collective-permute-done.43 = bf16[2,1,1,1,2,1,24,768]{7,6,0,5,4,3,2,1:T(8,128)(2,1)S(1)} collective-permute-done((bf16[2,1,1,1,2,1,24,768]{7,6,0,5,4,3,2,1:T(8,128)(2,1)S(1)}, bf16[2,1,1,1,2,1,24,768]{7,6,0,5,4,3,2,1:T(8,128)(2,1)S(1)}, u32[]{:S(2)}, u32[]{:S(2)}) %collective-permute-start.43) | collective-permute-done | bytes 147488 | tf_op jit(solution)/shard_map/ppermute | solution.py:683
  435.1 1.6 collective-permute-done.39
  439.2 1.9 collective-permute-start.57
  441.2 1.7 multiply_reduce_fusion
  442.9 7.2 %collective-permute-done.57 = bf16[2,2,1,1,1,64,768]{6,5,4,3,2,1,0:T(8,128)(2,1)S(1)} collective-permute-done((bf16[2,2,1,1,1,64,768]{6,5,4,3,2,1,0:T(8,128)(2,1)S(1)}, bf16[2,2,1,1,1,64,768]{6,5,4,3,2,1,0:T(8,128)(2,1)S(1)}, u32[]{:S(2)}, u32[]{:S(2)}) %collective-permute-start.57) | collective-permute-done | bytes 393248 | tf_op jit(solution)/shard_map/ppermute | solution.py:683
  450.5 2.5 collective-permute-start.58
  453.2 8.2 %collective-permute-done.58 = bf16[1,2,1,1,1,64,768]{6,5,4,3,2,1,0:T(8,128)(2,1)S(1)} collective-permute-done((bf16[1,2,1,1,1,64,768]{6,5,4,3,2,1,0:T(8,128)(2,1)S(1)}, bf16[1,2,1,1,1,64,768]{6,5,4,3,2,1,0:T(8,128)(2,1)S(1)}, u32[]{:S(2)}, u32[]{:S(2)}) %collective-permute-start.58) | collective-permute-done | bytes 196640 | tf_op jit(solution)/shard_map/ppermute | solution.py:683
  462.1 4.0 collective-permute-done.59
  469.5 2.1 collective-permute-start.60
  471.6 2.1 collective-permute-done.60
  475.1 2.3 collective-permute-start.62
  477.4 3.0 fusion.5
  482.7 2.9 collective-permute-done.63
  486.3 3.6 collective-permute-done.64
  (318 shorter events, 77.7 us)
Async XLA Ops:
  7.2 181.2 %all-gather.2.cloned.1.call-start = ((), (), s32[]{:S(2)}) async-start(), calls=%async_computation.1 | async-start | bytes 6488064 | tf_op jit(solution)/shard_map/all_gather | solution.py:746
  7.3 25.0 %collective-permute-start.26 = (bf16[1,1,1,1,1,64,768]{6,5,4,3,2,1,0:T(8,128)(2,1)}, bf16[1,1,1,1,1,64,768]{6,5,4,3,2,1,0:T(8,128)(2,1)S(1)}, u32[]{:S(2)}, u32[]{:S(2)}) collective-permute-start(bf16[1,1,1,1,1,64,768]{6,5,4,3,2,1,0:T(8,128)(2,1)} %bitcast.194), channel_id=1, source_target_pairs={{0,16},{4,20},{8,24},{12,28},{16,0},{20,4},{24,8},{28,12},{1,17},{... | collective-permute-start | bytes 294920 | tf_op jit(solution)/shard_map/ppermute | solution.py:683
  12.3 13.8 %collective-permute-start.4 = (bf16[2,1,1,1,1,1,24,768]{7,6,0,5,4,3,2,1:T(8,128)(2,1)S(1)}, bf16[2,1,1,1,1,1,24,768]{7,6,0,5,4,3,2,1:T(8,128)(2,1)S(1)}, u32[]{:S(2)}, u32[]{:S(2)}) collective-permute-start(bf16[2,1,1,1,1,1,24,768]{7,6,0,5,4,3,2,1:T(8,128)(2,1)S(1)} %get-tuple-element.198), channel_id=1, source_target_pairs={{0,16},{4,20},{8,24},{12,28},{16,0},{20,4},{24,8},{28,12},{1,17},{... | collective-permute-start | bytes 221192 | tf_op jit(solution)/shard_map/ppermute | solution.py:683
  12.4 14.2 %collective-permute-start.9 = (bf16[2,1,1,1,1,1,24,768]{7,6,0,5,4,3,2,1:T(8,128)(2,1)S(1)}, bf16[2,1,1,1,1,1,24,768]{7,6,0,5,4,3,2,1:T(8,128)(2,1)S(1)}, u32[]{:S(2)}, u32[]{:S(2)}) collective-permute-start(bf16[2,1,1,1,1,1,24,768]{7,6,0,5,4,3,2,1:T(8,128)(2,1)S(1)} %get-tuple-element.197), channel_id=1, source_target_pairs={{0,2},{1,3},{2,0},{3,1},{4,6},{5,7},{6,4},{7,5},{8,10},{9,11},{10,... | collective-permute-start | bytes 221192 | tf_op jit(solution)/shard_map/ppermute | solution.py:683
  15.2 14.0 %collective-permute-start.16 = (bf16[2,1,1,1,1,1,24,768]{7,6,0,5,4,3,2,1:T(8,128)(2,1)S(1)}, bf16[2,1,1,1,1,1,24,768]{7,6,0,5,4,3,2,1:T(8,128)(2,1)S(1)}, u32[]{:S(2)}, u32[]{:S(2)}) collective-permute-start(bf16[2,1,1,1,1,1,24,768]{7,6,0,5,4,3,2,1:T(8,128)(2,1)S(1)} %get-tuple-element.194), channel_id=1, source_target_pairs={{0,16},{4,20},{8,24},{12,28},{16,0},{20,4},{24,8},{28,12},{1,17},{... | collective-permute-start | bytes 221192 | tf_op jit(solution)/shard_map/ppermute | solution.py:683
  18.6 4.2 collective-permute-start
  19.2 447.8 %reduce-scatter.4.cloned.1.call-start = ((), (), s32[]{:S(2)}) async-start(), calls=%async_computation.2 | async-start | bytes 6488064
  24.0 5.5 %collective-permute-start.21 = (bf16[2,1,1,1,1,1,24,768]{7,6,0,5,4,3,2,1:T(8,128)(2,1)S(1)}, bf16[2,1,1,1,1,1,24,768]{7,6,0,5,4,3,2,1:T(8,128)(2,1)S(1)}, u32[]{:S(2)}, u32[]{:S(2)}) collective-permute-start(bf16[2,1,1,1,1,1,24,768]{7,6,0,5,4,3,2,1:T(8,128)(2,1)S(1)} %get-tuple-element.193), channel_id=1, source_target_pairs={{0,2},{1,3},{2,0},{3,1},{4,6},{5,7},{6,4},{7,5},{8,10},{9,11},{10,... | collective-permute-start | bytes 221192 | tf_op jit(solution)/shard_map/ppermute | solution.py:683
  26.1 65.1 %collective-permute-start.2 = (bf16[2,1,1,256,768]{4,3,0,2,1:T(8,128)(2,1)}, bf16[2,1,1,256,768]{4,3,0,2,1:T(8,128)(2,1)S(1)}, u32[]{:S(2)}, u32[]{:S(2)}) collective-permute-start(bf16[2,1,1,256,768]{4,3,0,2,1:T(8,128)(2,1)} %bitcast.147), channel_id=1, source_target_pairs={{0,2},{1,3},{2,0},{3,1},{4,6},{5,7},{6,4},{7,5},{8,10},{9,11},{10,... | collective-permute-start | bytes 2359304 | tf_op jit(solution)/shard_map/ppermute | solution.py:683
  26.6 37.2 %collective-permute-start.14 = (bf16[2,1,1,128,768]{4,3,0,2,1:T(8,128)(2,1)}, bf16[2,1,1,128,768]{4,3,0,2,1:T(8,128)(2,1)S(1)}, u32[]{:S(2)}, u32[]{:S(2)}) collective-permute-start(bf16[2,1,1,128,768]{4,3,0,2,1:T(8,128)(2,1)} %bitcast.193), channel_id=1, source_target_pairs={{0,2},{1,3},{2,0},{3,1},{4,6},{5,7},{6,4},{7,5},{8,10},{9,11},{10,... | collective-permute-start | bytes 1179656 | tf_op jit(solution)/shard_map/ppermute | solution.py:683
  29.1 16.5 %collective-permute-start.10 = (bf16[2,1,1,1,2,1,24,768]{7,6,0,5,4,3,2,1:T(8,128)(2,1)S(1)}, bf16[2,1,1,1,2,1,24,768]{7,6,0,5,4,3,2,1:T(8,128)(2,1)S(1)}, u32[]{:S(2)}, u32[]{:S(2)}) collective-permute-start(bf16[2,1,1,1,2,1,24,768]{7,6,0,5,4,3,2,1:T(8,128)(2,1)S(1)} %pad_maximum_fusion.29), channel_id=1, source_target_pairs={{0,16},{4,20},{8,24},{12,28},{16,0},{20,4},{24,8},{28,12},{1,17},{... | collective-permute-start | bytes 442376 | tf_op jit(solution)/shard_map/ppermute | solution.py:683
  29.6 18.5 %collective-permute-start.22 = (bf16[2,1,1,1,2,1,24,768]{7,6,0,5,4,3,2,1:T(8,128)(2,1)S(1)}, bf16[2,1,1,1,2,1,24,768]{7,6,0,5,4,3,2,1:T(8,128)(2,1)S(1)}, u32[]{:S(2)}, u32[]{:S(2)}) collective-permute-start(bf16[2,1,1,1,2,1,24,768]{7,6,0,5,4,3,2,1:T(8,128)(2,1)S(1)} %pad_maximum_fusion.31), channel_id=1, source_target_pairs={{0,16},{4,20},{8,24},{12,28},{16,0},{20,4},{24,8},{28,12},{1,17},{... | collective-permute-start | bytes 442376 | tf_op jit(solution)/shard_map/ppermute | solution.py:683
  32.3 15.9 %collective-permute-start.5 = (bf16[2,2,1,1,1,1,24,768]{7,6,0,5,4,3,2,1:T(8,128)(2,1)S(1)}, bf16[2,2,1,1,1,1,24,768]{7,6,0,5,4,3,2,1:T(8,128)(2,1)S(1)}, u32[]{:S(2)}, u32[]{:S(2)}) collective-permute-start(bf16[2,2,1,1,1,1,24,768]{7,6,0,5,4,3,2,1:T(8,128)(2,1)S(1)} %pad_maximum_fusion.28), channel_id=1, source_target_pairs={{0,8},{4,12},{8,0},{12,4},{16,24},{20,28},{24,16},{28,20},{1,9},{5... | collective-permute-start | bytes 442376 | tf_op jit(solution)/shard_map/ppermute | solution.py:683
  45.6 8.6 %collective-permute-start.17 = (bf16[2,2,1,1,1,1,24,768]{7,6,0,5,4,3,2,1:T(8,128)(2,1)S(1)}, bf16[2,2,1,1,1,1,24,768]{7,6,0,5,4,3,2,1:T(8,128)(2,1)S(1)}, u32[]{:S(2)}, u32[]{:S(2)}) collective-permute-start(bf16[2,2,1,1,1,1,24,768]{7,6,0,5,4,3,2,1:T(8,128)(2,1)S(1)} %pad_maximum_fusion.30), channel_id=1, source_target_pairs={{0,8},{4,12},{8,0},{12,4},{16,24},{20,28},{24,16},{28,20},{1,9},{5... | collective-permute-start | bytes 442376 | tf_op jit(solution)/shard_map/ppermute | solution.py:683
  48.1 14.2 %collective-permute-start.27 = (bf16[2,1,1,1,1,64,768]{6,5,4,3,2,1,0:T(8,128)(2,1)S(1)}, bf16[2,1,1,1,1,64,768]{6,5,4,3,2,1,0:T(8,128)(2,1)S(1)}, u32[]{:S(2)}, u32[]{:S(2)}) collective-permute-start(bf16[2,1,1,1,1,64,768]{6,5,4,3,2,1,0:T(8,128)(2,1)S(1)} %pad_maximum_fusion.27), channel_id=1, source_target_pairs={{0,8},{4,12},{8,0},{12,4},{16,24},{20,28},{24,16},{28,20},{1,9},{5... | collective-permute-start | bytes 589832 | tf_op jit(solution)/shard_map/ppermute | solution.py:683
  48.2 23.1 %collective-permute-start.11 = (bf16[2,2,1,1,2,1,24,768]{7,6,0,5,4,3,2,1:T(8,128)(2,1)S(1)}, bf16[2,2,1,1,2,1,24,768]{7,6,0,5,4,3,2,1:T(8,128)(2,1)S(1)}, u32[]{:S(2)}, u32[]{:S(2)}) collective-permute-start(bf16[2,2,1,1,2,1,24,768]{7,6,0,5,4,3,2,1:T(8,128)(2,1)S(1)} %pad_maximum_fusion.22), channel_id=1, source_target_pairs={{0,8},{4,12},{8,0},{12,4},{16,24},{20,28},{24,16},{28,20},{1,9},{5... | collective-permute-start | bytes 884744 | tf_op jit(solution)/shard_map/ppermute | solution.py:683
  54.2 22.3 %collective-permute-start.23 = (bf16[2,2,1,1,2,1,24,768]{7,6,0,5,4,3,2,1:T(8,128)(2,1)S(1)}, bf16[2,2,1,1,2,1,24,768]{7,6,0,5,4,3,2,1:T(8,128)(2,1)S(1)}, u32[]{:S(2)}, u32[]{:S(2)}) collective-permute-start(bf16[2,2,1,1,2,1,24,768]{7,6,0,5,4,3,2,1:T(8,128)(2,1)S(1)} %pad_maximum_fusion.24), channel_id=1, source_target_pairs={{0,8},{4,12},{8,0},{12,4},{16,24},{20,28},{24,16},{28,20},{1,9},{5... | collective-permute-start | bytes 884744 | tf_op jit(solution)/shard_map/ppermute | solution.py:683
  62.3 14.3 %collective-permute-start.6 = (bf16[2,2,2,1,1,1,24,768]{7,6,0,5,4,3,2,1:T(8,128)(2,1)S(1)}, bf16[2,2,2,1,1,1,24,768]{7,6,0,5,4,3,2,1:T(8,128)(2,1)S(1)}, u32[]{:S(2)}, u32[]{:S(2)}) collective-permute-start(bf16[2,2,2,1,1,1,24,768]{7,6,0,5,4,3,2,1:T(8,128)(2,1)S(1)} %pad_maximum_fusion.21), channel_id=1, source_target_pairs={{0,4},{4,0},{8,12},{12,8},{16,20},{20,16},{24,28},{28,24},{1,5},{5... | collective-permute-start | bytes 884744 | tf_op jit(solution)/shard_map/ppermute | solution.py:683
  63.8 14.5 %collective-permute-start.18 = (bf16[2,2,2,1,1,1,24,768]{7,6,0,5,4,3,2,1:T(8,128)(2,1)S(1)}, bf16[2,2,2,1,1,1,24,768]{7,6,0,5,4,3,2,1:T(8,128)(2,1)S(1)}, u32[]{:S(2)}, u32[]{:S(2)}) collective-permute-start(bf16[2,2,2,1,1,1,24,768]{7,6,0,5,4,3,2,1:T(8,128)(2,1)S(1)} %pad_maximum_fusion.23), channel_id=1, source_target_pairs={{0,4},{4,0},{8,12},{12,8},{16,20},{20,16},{24,28},{28,24},{1,5},{5... | collective-permute-start | bytes 884744 | tf_op jit(solution)/shard_map/ppermute | solution.py:683
  71.3 18.9 %collective-permute-start.28 = (bf16[2,2,1,1,1,64,768]{6,5,4,3,2,1,0:T(8,128)(2,1)S(1)}, bf16[2,2,1,1,1,64,768]{6,5,4,3,2,1,0:T(8,128)(2,1)S(1)}, u32[]{:S(2)}, u32[]{:S(2)}) collective-permute-start(bf16[2,2,1,1,1,64,768]{6,5,4,3,2,1,0:T(8,128)(2,1)S(1)} %pad_maximum_fusion.20), channel_id=1, source_target_pairs={{0,4},{4,0},{8,12},{12,8},{16,20},{20,16},{24,28},{28,24},{1,5},{5... | collective-permute-start | bytes 1179656 | tf_op jit(solution)/shard_map/ppermute | solution.py:683
  76.5 43.1 %collective-permute-start.15 = (bf16[2,2,1,128,768]{4,3,0,2,1:T(8,128)(2,1)S(1)}, bf16[2,2,1,128,768]{4,3,0,2,1:T(8,128)(2,1)S(1)}, u32[]{:S(2)}, u32[]{:S(2)}) collective-permute-start(bf16[2,2,1,128,768]{4,3,0,2,1:T(8,128)(2,1)S(1)} %pad_maximum_fusion.14), channel_id=1, source_target_pairs={{0,1},{1,0},{2,3},{3,2},{4,5},{5,4},{6,7},{7,6},{8,9},{9,8},{10,11... | collective-permute-start | bytes 2359304 | tf_op jit(solution)/shard_map/ppermute | solution.py:683
  76.6 30.7 %collective-permute-start.12 = (bf16[2,2,2,1,2,1,24,768]{7,6,0,5,4,3,2,1:T(8,128)(2,1)S(1)}, bf16[2,2,2,1,2,1,24,768]{7,6,0,5,4,3,2,1:T(8,128)(2,1)S(1)}, u32[]{:S(2)}, u32[]{:S(2)}) collective-permute-start(bf16[2,2,2,1,2,1,24,768]{7,6,0,5,4,3,2,1:T(8,128)(2,1)S(1)} %pad_maximum_fusion.17), channel_id=1, source_target_pairs={{0,4},{4,0},{8,12},{12,8},{16,20},{20,16},{24,28},{28,24},{1,5},{5... | collective-permute-start | bytes 1769480 | tf_op jit(solution)/shard_map/ppermute | solution.py:683
  78.3 39.9 %collective-permute-start.24 = (bf16[2,2,2,1,2,1,24,768]{7,6,0,5,4,3,2,1:T(8,128)(2,1)S(1)}, bf16[2,2,2,1,2,1,24,768]{7,6,0,5,4,3,2,1:T(8,128)(2,1)S(1)}, u32[]{:S(2)}, u32[]{:S(2)}) collective-permute-start(bf16[2,2,2,1,2,1,24,768]{7,6,0,5,4,3,2,1:T(8,128)(2,1)S(1)} %pad_maximum_fusion.19), channel_id=1, source_target_pairs={{0,4},{4,0},{8,12},{12,8},{16,20},{20,16},{24,28},{28,24},{1,5},{5... | collective-permute-start | bytes 1769480 | tf_op jit(solution)/shard_map/ppermute | solution.py:683
  90.2 28.3 %collective-permute-start.7 = (bf16[2,2,2,2,1,1,24,768]{7,6,0,5,4,3,2,1:T(8,128)(2,1)S(1)}, bf16[2,2,2,2,1,1,24,768]{7,6,0,5,4,3,2,1:T(8,128)(2,1)S(1)}, u32[]{:S(2)}, u32[]{:S(2)}) collective-permute-start(bf16[2,2,2,2,1,1,24,768]{7,6,0,5,4,3,2,1:T(8,128)(2,1)S(1)} %pad_maximum_fusion.16), channel_id=1, source_target_pairs={{0,2},{1,3},{2,0},{3,1},{4,6},{5,7},{6,4},{7,5},{8,10},{9,11},{10,... | collective-permute-start | bytes 1769480 | tf_op jit(solution)/shard_map/ppermute | solution.py:683
  91.2 27.9 %collective-permute-start.19 = (bf16[2,2,2,2,1,1,24,768]{7,6,0,5,4,3,2,1:T(8,128)(2,1)S(1)}, bf16[2,2,2,2,1,1,24,768]{7,6,0,5,4,3,2,1:T(8,128)(2,1)S(1)}, u32[]{:S(2)}, u32[]{:S(2)}) collective-permute-start(bf16[2,2,2,2,1,1,24,768]{7,6,0,5,4,3,2,1:T(8,128)(2,1)S(1)} %pad_maximum_fusion.18), channel_id=1, source_target_pairs={{0,2},{1,3},{2,0},{3,1},{4,6},{5,7},{6,4},{7,5},{8,10},{9,11},{10,... | collective-permute-start | bytes 1769480 | tf_op jit(solution)/shard_map/ppermute | solution.py:683
  107.3 22.9 %collective-permute-start.29 = (bf16[2,2,2,1,1,64,768]{6,5,4,3,2,1,0:T(8,128)(2,1)S(1)}, bf16[2,2,2,1,1,64,768]{6,5,4,3,2,1,0:T(8,128)(2,1)S(1)}, u32[]{:S(2)}, u32[]{:S(2)}) collective-permute-start(bf16[2,2,2,1,1,64,768]{6,5,4,3,2,1,0:T(8,128)(2,1)S(1)} %pad_maximum_fusion.15), channel_id=1, source_target_pairs={{0,2},{1,3},{2,0},{3,1},{4,6},{5,7},{6,4},{7,5},{8,10},{9,11},{10,... | collective-permute-start | bytes 2359304 | tf_op jit(solution)/shard_map/ppermute | solution.py:683
  118.2 21.8 %collective-permute-start.3 = (bf16[2,2,1,256,768]{4,3,0,2,1:T(8,128)(2,1)S(1)}, bf16[2,2,1,256,768]{4,3,0,2,1:T(8,128)(2,1)S(1)}, u32[]{:S(2)}, u32[]{:S(2)}) collective-permute-start(bf16[2,2,1,256,768]{4,3,0,2,1:T(8,128)(2,1)S(1)} %pad_maximum_fusion.7), channel_id=1, source_target_pairs={{0,1},{1,0},{2,3},{3,2},{4,5},{5,4},{6,7},{7,6},{8,9},{9,8},{10,11... | collective-permute-start | bytes 4718600 | tf_op jit(solution)/shard_map/ppermute | solution.py:683
  118.5 11.9 %collective-permute-start.13 = (bf16[2,2,2,2,2,1,24,768]{7,6,0,5,4,3,2,1:T(8,128)(2,1)S(1)}, bf16[2,2,2,2,2,1,24,768]{7,6,0,5,4,3,2,1:T(8,128)(2,1)S(1)}, u32[]{:S(2)}, u32[]{:S(2)}) collective-permute-start(bf16[2,2,2,2,2,1,24,768]{7,6,0,5,4,3,2,1:T(8,128)(2,1)S(1)} %pad_maximum_fusion.11), channel_id=1, source_target_pairs={{0,1},{1,0},{2,3},{3,2},{4,5},{5,4},{6,7},{7,6},{8,9},{9,8},{10,11... | collective-permute-start | bytes 3538952 | tf_op jit(solution)/shard_map/ppermute | solution.py:683
  119.1 11.9 %collective-permute-start.25 = (bf16[2,2,2,2,2,1,24,768]{7,6,0,5,4,3,2,1:T(8,128)(2,1)S(1)}, bf16[2,2,2,2,2,1,24,768]{7,6,0,5,4,3,2,1:T(8,128)(2,1)S(1)}, u32[]{:S(2)}, u32[]{:S(2)}) collective-permute-start(bf16[2,2,2,2,2,1,24,768]{7,6,0,5,4,3,2,1:T(8,128)(2,1)S(1)} %pad_maximum_fusion.13), channel_id=1, source_target_pairs={{0,1},{1,0},{2,3},{3,2},{4,5},{5,4},{6,7},{7,6},{8,9},{9,8},{10,11... | collective-permute-start | bytes 3538952 | tf_op jit(solution)/shard_map/ppermute | solution.py:683
  119.6 11.9 %collective-permute-start.20 = (bf16[2,2,2,2,2,1,24,768]{7,6,0,5,4,3,2,1:T(8,128)(2,1)S(1)}, bf16[2,2,2,2,2,1,24,768]{7,6,0,5,4,3,2,1:T(8,128)(2,1)S(1)}, u32[]{:S(2)}, u32[]{:S(2)}) collective-permute-start(bf16[2,2,2,2,2,1,24,768]{7,6,0,5,4,3,2,1:T(8,128)(2,1)S(1)} %pad_maximum_fusion.12), channel_id=1, source_target_pairs={{0,1},{1,0},{2,3},{3,2},{4,5},{5,4},{6,7},{7,6},{8,9},{9,8},{10,11... | collective-permute-start | bytes 3538952 | tf_op jit(solution)/shard_map/ppermute | solution.py:683
  130.4 54.2 %collective-permute-start.30 = (bf16[2,2,2,2,1,64,768]{6,5,4,3,2,1,0:T(8,128)(2,1)S(1)}, bf16[2,2,2,2,1,64,768]{6,5,4,3,2,1,0:T(8,128)(2,1)}, u32[]{:S(2)}, u32[]{:S(2)}) collective-permute-start(bf16[2,2,2,2,1,64,768]{6,5,4,3,2,1,0:T(8,128)(2,1)S(1)} %pad_maximum_fusion.9), channel_id=1, source_target_pairs={{0,1},{1,0},{2,3},{3,2},{4,5},{5,4},{6,7},{7,6},{8,9},{9,8},{10,11... | collective-permute-start | bytes 4718600 | tf_op jit(solution)/shard_map/ppermute | solution.py:683
  286.1 53.3 %collective-permute-start.31 = (bf16[2,2,1,256,768]{4,3,0,2,1:T(8,128)(2,1)}, bf16[2,2,1,256,768]{4,3,0,2,1:T(8,128)(2,1)}, u32[]{:S(2)}, u32[]{:S(2)}) collective-permute-start(bf16[2,2,1,256,768]{4,3,0,2,1:T(8,128)(2,1)} %copy.92), channel_id=1, source_target_pairs={{0,1},{1,0},{2,3},{3,2},{4,5},{5,4},{6,7},{7,6},{8,9},{9,8},{10,11... | collective-permute-start | bytes 4718600 | tf_op jit(solution)/shard_map/ppermute | solution.py:683
  288.7 56.4 %collective-permute-start.55 = (bf16[2,2,2,2,1,64,768]{6,5,4,3,2,1,0:T(8,128)(2,1)}, bf16[2,2,2,2,1,64,768]{6,5,4,3,2,1,0:T(8,128)(2,1)}, u32[]{:S(2)}, u32[]{:S(2)}) collective-permute-start(bf16[2,2,2,2,1,64,768]{6,5,4,3,2,1,0:T(8,128)(2,1)} %constant_dynamic-slice_fusion.4), channel_id=1, source_target_pairs={{0,1},{1,0},{2,3},{3,2},{4,5},{5,4},{6,7},{7,6},{8,9},{9,8},{10,11... | collective-permute-start | bytes 4718600 | tf_op jit(solution)/shard_map/ppermute | solution.py:683
  290.7 33.6 %collective-permute-start.45 = (bf16[2,2,2,2,2,1,24,768]{7,6,0,5,4,3,2,1:T(8,128)(2,1)}, bf16[2,2,2,2,2,1,24,768]{7,6,0,5,4,3,2,1:T(8,128)(2,1)}, u32[]{:S(2)}, u32[]{:S(2)}) collective-permute-start(bf16[2,2,2,2,2,1,24,768]{7,6,0,5,4,3,2,1:T(8,128)(2,1)} %fusion.9), channel_id=1, source_target_pairs={{0,1},{1,0},{2,3},{3,2},{4,5},{5,4},{6,7},{7,6},{8,9},{9,8},{10,11... | collective-permute-start | bytes 3538952 | tf_op jit(solution)/shard_map/ppermute | solution.py:683
  291.9 30.5 %collective-permute-start.33 = (bf16[2,2,1,128,768]{4,3,0,2,1:T(8,128)(2,1)}, bf16[2,2,1,128,768]{4,3,0,2,1:T(8,128)(2,1)}, u32[]{:S(2)}, u32[]{:S(2)}) collective-permute-start(bf16[2,2,1,128,768]{4,3,0,2,1:T(8,128)(2,1)} %copy.94), channel_id=1, source_target_pairs={{0,1},{1,0},{2,3},{3,2},{4,5},{5,4},{6,7},{7,6},{8,9},{9,8},{10,11... | collective-permute-start | bytes 2359304 | tf_op jit(solution)/shard_map/ppermute | solution.py:683
  316.1 10.3 %collective-permute-start.35 = (bf16[2,2,2,2,2,1,24,768]{7,6,0,5,4,3,2,1:T(8,128)(2,1)}, bf16[2,2,2,2,2,1,24,768]{7,6,0,5,4,3,2,1:T(8,128)(2,1)}, u32[]{:S(2)}, u32[]{:S(2)}) collective-permute-start(bf16[2,2,2,2,2,1,24,768]{7,6,0,5,4,3,2,1:T(8,128)(2,1)} %fusion.13), channel_id=1, source_target_pairs={{0,1},{1,0},{2,3},{3,2},{4,5},{5,4},{6,7},{7,6},{8,9},{9,8},{10,11... | collective-permute-start | bytes 3538952 | tf_op jit(solution)/shard_map/ppermute | solution.py:683
  322.4 7.0 %collective-permute-start.50 = (bf16[2,2,2,2,2,1,24,768]{7,6,0,5,4,3,2,1:T(8,128)(2,1)S(1)}, bf16[2,2,2,2,2,1,24,768]{7,6,0,5,4,3,2,1:T(8,128)(2,1)S(1)}, u32[]{:S(2)}, u32[]{:S(2)}) collective-permute-start(bf16[2,2,2,2,2,1,24,768]{7,6,0,5,4,3,2,1:T(8,128)(2,1)S(1)} %fusion.7), channel_id=1, source_target_pairs={{0,1},{1,0},{2,3},{3,2},{4,5},{5,4},{6,7},{7,6},{8,9},{9,8},{10,11... | collective-permute-start | bytes 3538952 | tf_op jit(solution)/shard_map/ppermute | solution.py:683
  324.2 6.7 %collective-permute-start.40 = (bf16[2,2,2,2,2,1,24,768]{7,6,0,5,4,3,2,1:T(8,128)(2,1)S(1)}, bf16[2,2,2,2,2,1,24,768]{7,6,0,5,4,3,2,1:T(8,128)(2,1)S(1)}, u32[]{:S(2)}, u32[]{:S(2)}) collective-permute-start(bf16[2,2,2,2,2,1,24,768]{7,6,0,5,4,3,2,1:T(8,128)(2,1)S(1)} %fusion.11), channel_id=1, source_target_pairs={{0,1},{1,0},{2,3},{3,2},{4,5},{5,4},{6,7},{7,6},{8,9},{9,8},{10,11... | collective-permute-start | bytes 3538952 | tf_op jit(solution)/shard_map/ppermute | solution.py:683
  326.4 12.0 %collective-permute-start.34 = (bf16[2,1,1,128,768]{4,3,0,2,1:T(8,128)(2,1)S(1)}, bf16[2,1,1,128,768]{4,3,0,2,1:T(8,128)(2,1)S(1)}, u32[]{:S(2)}, u32[]{:S(2)}) collective-permute-start(bf16[2,1,1,128,768]{4,3,0,2,1:T(8,128)(2,1)S(1)} %constant_dynamic-slice_fusion.21), channel_id=1, source_target_pairs={{0,2},{1,3},{2,0},{3,1},{4,6},{5,7},{6,4},{7,5},{8,10},{9,11},{10,... | collective-permute-start | bytes 1179656 | tf_op jit(solution)/shard_map/ppermute | solution.py:683
  329.3 21.7 %collective-permute-start.46 = (bf16[2,2,2,2,1,1,24,768]{7,6,0,5,4,3,2,1:T(8,128)(2,1)S(1)}, bf16[2,2,2,2,1,1,24,768]{7,6,0,5,4,3,2,1:T(8,128)(2,1)S(1)}, u32[]{:S(2)}, u32[]{:S(2)}) collective-permute-start(bf16[2,2,2,2,1,1,24,768]{7,6,0,5,4,3,2,1:T(8,128)(2,1)S(1)} %constant_dynamic-slice_fusion.12), channel_id=1, source_target_pairs={{0,2},{1,3},{2,0},{3,1},{4,6},{5,7},{6,4},{7,5},{8,10},{9,11},{10,... | collective-permute-start | bytes 1769480 | tf_op jit(solution)/shard_map/ppermute | solution.py:683
  330.9 20.4 %collective-permute-start.51 = (bf16[2,2,2,1,2,1,24,768]{7,6,0,5,4,3,2,1:T(8,128)(2,1)S(1)}, bf16[2,2,2,1,2,1,24,768]{7,6,0,5,4,3,2,1:T(8,128)(2,1)S(1)}, u32[]{:S(2)}, u32[]{:S(2)}) collective-permute-start(bf16[2,2,2,1,2,1,24,768]{7,6,0,5,4,3,2,1:T(8,128)(2,1)S(1)} %constant_dynamic-slice_fusion.8), channel_id=1, source_target_pairs={{0,4},{4,0},{8,12},{12,8},{16,20},{20,16},{24,28},{28,24},{1,5},{5... | collective-permute-start | bytes 1769480 | tf_op jit(solution)/shard_map/ppermute | solution.py:683
  338.4 25.3 %collective-permute-start.36 = (bf16[2,2,2,2,1,1,24,768]{7,6,0,5,4,3,2,1:T(8,128)(2,1)S(1)}, bf16[2,2,2,2,1,1,24,768]{7,6,0,5,4,3,2,1:T(8,128)(2,1)S(1)}, u32[]{:S(2)}, u32[]{:S(2)}) collective-permute-start(bf16[2,2,2,2,1,1,24,768]{7,6,0,5,4,3,2,1:T(8,128)(2,1)S(1)} %constant_dynamic-slice_fusion.20), channel_id=1, source_target_pairs={{0,2},{1,3},{2,0},{3,1},{4,6},{5,7},{6,4},{7,5},{8,10},{9,11},{10,... | collective-permute-start | bytes 1769480 | tf_op jit(solution)/shard_map/ppermute | solution.py:683
  339.5 26.8 %collective-permute-start.41 = (bf16[2,2,2,1,2,1,24,768]{7,6,0,5,4,3,2,1:T(8,128)(2,1)S(1)}, bf16[2,2,2,1,2,1,24,768]{7,6,0,5,4,3,2,1:T(8,128)(2,1)S(1)}, u32[]{:S(2)}, u32[]{:S(2)}) collective-permute-start(bf16[2,2,2,1,2,1,24,768]{7,6,0,5,4,3,2,1:T(8,128)(2,1)S(1)} %constant_dynamic-slice_fusion.16), channel_id=1, source_target_pairs={{0,4},{4,0},{8,12},{12,8},{16,20},{20,16},{24,28},{28,24},{1,5},{5... | collective-permute-start | bytes 1769480 | tf_op jit(solution)/shard_map/ppermute | solution.py:683
  345.1 96.1 %collective-permute-start.32 = (bf16[2,1,1,256,768]{4,3,0,2,1:T(8,128)(2,1)}, bf16[2,1,1,256,768]{4,3,0,2,1:T(8,128)(2,1)}, u32[]{:S(2)}, u32[]{:S(2)}) collective-permute-start(bf16[2,1,1,256,768]{4,3,0,2,1:T(8,128)(2,1)} %constant_dynamic-slice_fusion.24), channel_id=1, source_target_pairs={{0,2},{1,3},{2,0},{3,1},{4,6},{5,7},{6,4},{7,5},{8,10},{9,11},{10,... | collective-permute-start | bytes 2359304 | tf_op jit(solution)/shard_map/ppermute | solution.py:683
  351.0 87.7 %collective-permute-start.56 = (bf16[2,2,2,1,1,64,768]{6,5,4,3,2,1,0:T(8,128)(2,1)}, bf16[2,2,2,1,1,64,768]{6,5,4,3,2,1,0:T(8,128)(2,1)S(1)}, u32[]{:S(2)}, u32[]{:S(2)}) collective-permute-start(bf16[2,2,2,1,1,64,768]{6,5,4,3,2,1,0:T(8,128)(2,1)} %constant_dynamic-slice_fusion.3), channel_id=1, source_target_pairs={{0,2},{1,3},{2,0},{3,1},{4,6},{5,7},{6,4},{7,5},{8,10},{9,11},{10,... | collective-permute-start | bytes 2359304 | tf_op jit(solution)/shard_map/ppermute | solution.py:683
  351.3 16.7 %collective-permute-start.47 = (bf16[2,2,2,1,1,1,24,768]{7,6,0,5,4,3,2,1:T(8,128)(2,1)S(1)}, bf16[2,2,2,1,1,1,24,768]{7,6,0,5,4,3,2,1:T(8,128)(2,1)S(1)}, u32[]{:S(2)}, u32[]{:S(2)}) collective-permute-start(bf16[2,2,2,1,1,1,24,768]{7,6,0,5,4,3,2,1:T(8,128)(2,1)S(1)} %constant_dynamic-slice_fusion.11), channel_id=1, source_target_pairs={{0,4},{4,0},{8,12},{12,8},{16,20},{20,16},{24,28},{28,24},{1,5},{5... | collective-permute-start | bytes 884744 | tf_op jit(solution)/shard_map/ppermute | solution.py:683
  363.7 36.5 %collective-permute-start.52 = (bf16[2,1,2,1,2,1,24,768]{7,6,0,5,4,3,2,1:T(8,128)(2,1)S(1)}, bf16[2,1,2,1,2,1,24,768]{7,6,0,5,4,3,2,1:T(8,128)(2,1)S(1)}, u32[]{:S(2)}, u32[]{:S(2)}) collective-permute-start(bf16[2,1,2,1,2,1,24,768]{7,6,0,5,4,3,2,1:T(8,128)(2,1)S(1)} %constant_dynamic-slice_fusion.7), channel_id=1, source_target_pairs={{0,16},{4,20},{8,24},{12,28},{16,0},{20,4},{24,8},{28,12},{1,17},{... | collective-permute-start | bytes 884744 | tf_op jit(solution)/shard_map/ppermute | solution.py:683
  366.3 34.0 %collective-permute-start.37 = (bf16[2,2,2,1,1,1,24,768]{7,6,0,5,4,3,2,1:T(8,128)(2,1)S(1)}, bf16[2,2,2,1,1,1,24,768]{7,6,0,5,4,3,2,1:T(8,128)(2,1)S(1)}, u32[]{:S(2)}, u32[]{:S(2)}) collective-permute-start(bf16[2,2,2,1,1,1,24,768]{7,6,0,5,4,3,2,1:T(8,128)(2,1)S(1)} %constant_dynamic-slice_fusion.19), channel_id=1, source_target_pairs={{0,4},{4,0},{8,12},{12,8},{16,20},{20,16},{24,28},{28,24},{1,5},{5... | collective-permute-start | bytes 884744 | tf_op jit(solution)/shard_map/ppermute | solution.py:683
  368.0 44.5 %collective-permute-start.42 = (bf16[2,1,2,1,2,1,24,768]{7,6,0,5,4,3,2,1:T(8,128)(2,1)S(1)}, bf16[2,1,2,1,2,1,24,768]{7,6,0,5,4,3,2,1:T(8,128)(2,1)S(1)}, u32[]{:S(2)}, u32[]{:S(2)}) collective-permute-start(bf16[2,1,2,1,2,1,24,768]{7,6,0,5,4,3,2,1:T(8,128)(2,1)S(1)} %constant_dynamic-slice_fusion.15), channel_id=1, source_target_pairs={{0,16},{4,20},{8,24},{12,28},{16,0},{20,4},{24,8},{28,12},{1,17},{... | collective-permute-start | bytes 884744 | tf_op jit(solution)/shard_map/ppermute | solution.py:683
  400.2 18.5 %collective-permute-start.48 = (bf16[2,1,2,1,1,1,24,768]{7,6,0,5,4,3,2,1:T(8,128)(2,1)S(1)}, bf16[2,1,2,1,1,1,24,768]{7,6,0,5,4,3,2,1:T(8,128)(2,1)S(1)}, u32[]{:S(2)}, u32[]{:S(2)}) collective-permute-start(bf16[2,1,2,1,1,1,24,768]{7,6,0,5,4,3,2,1:T(8,128)(2,1)S(1)} %constant_dynamic-slice_fusion.10), channel_id=1, source_target_pairs={{0,16},{4,20},{8,24},{12,28},{16,0},{20,4},{24,8},{28,12},{1,17},{... | collective-permute-start | bytes 442376 | tf_op jit(solution)/shard_map/ppermute | solution.py:683
  400.3 19.3 %collective-permute-start.53 = (bf16[2,1,1,1,2,1,24,768]{7,6,0,5,4,3,2,1:T(8,128)(2,1)S(1)}, bf16[2,1,1,1,2,1,24,768]{7,6,0,5,4,3,2,1:T(8,128)(2,1)S(1)}, u32[]{:S(2)}, u32[]{:S(2)}) collective-permute-start(bf16[2,1,1,1,2,1,24,768]{7,6,0,5,4,3,2,1:T(8,128)(2,1)S(1)} %constant_dynamic-slice_fusion.6), channel_id=1, source_target_pairs={{0,8},{4,12},{8,0},{12,4},{16,24},{20,28},{24,16},{28,20},{1,9},{5... | collective-permute-start | bytes 442376 | tf_op jit(solution)/shard_map/ppermute | solution.py:683
  412.5 13.3 %collective-permute-start.38 = (bf16[2,1,2,1,1,1,24,768]{7,6,0,5,4,3,2,1:T(8,128)(2,1)S(1)}, bf16[2,1,2,1,1,1,24,768]{7,6,0,5,4,3,2,1:T(8,128)(2,1)S(1)}, u32[]{:S(2)}, u32[]{:S(2)}) collective-permute-start(bf16[2,1,2,1,1,1,24,768]{7,6,0,5,4,3,2,1:T(8,128)(2,1)S(1)} %constant_dynamic-slice_fusion.18), channel_id=1, source_target_pairs={{0,16},{4,20},{8,24},{12,28},{16,0},{20,4},{24,8},{28,12},{1,17},{... | collective-permute-start | bytes 442376 | tf_op jit(solution)/shard_map/ppermute | solution.py:683
  418.7 13.6 %collective-permute-start.43 = (bf16[2,1,1,1,2,1,24,768]{7,6,0,5,4,3,2,1:T(8,128)(2,1)S(1)}, bf16[2,1,1,1,2,1,24,768]{7,6,0,5,4,3,2,1:T(8,128)(2,1)S(1)}, u32[]{:S(2)}, u32[]{:S(2)}) collective-permute-start(bf16[2,1,1,1,2,1,24,768]{7,6,0,5,4,3,2,1:T(8,128)(2,1)S(1)} %constant_dynamic-slice_fusion.14), channel_id=1, source_target_pairs={{0,8},{4,12},{8,0},{12,4},{16,24},{20,28},{24,16},{28,20},{1,9},{5... | collective-permute-start | bytes 442376 | tf_op jit(solution)/shard_map/ppermute | solution.py:683
  419.6 13.9 %collective-permute-start.49 = (bf16[2,1,1,1,1,1,24,768]{7,6,0,5,4,3,2,1:T(8,128)(2,1)S(1)}, bf16[2,1,1,1,1,1,24,768]{7,6,0,5,4,3,2,1:T(8,128)(2,1)S(1)}, u32[]{:S(2)}, u32[]{:S(2)}) collective-permute-start(bf16[2,1,1,1,1,1,24,768]{7,6,0,5,4,3,2,1:T(8,128)(2,1)S(1)} %constant_dynamic-slice_fusion.9), channel_id=1, source_target_pairs={{0,8},{4,12},{8,0},{12,4},{16,24},{20,28},{24,16},{28,20},{1,9},{5... | collective-permute-start | bytes 221192 | tf_op jit(solution)/shard_map/ppermute | solution.py:683
  425.8 8.5 %collective-permute-start.54 = (bf16[2,1,1,1,1,1,24,768]{7,6,0,5,4,3,2,1:T(8,128)(2,1)S(1)}, bf16[2,1,1,1,1,1,24,768]{7,6,0,5,4,3,2,1:T(8,128)(2,1)S(1)}, u32[]{:S(2)}, u32[]{:S(2)}) collective-permute-start(bf16[2,1,1,1,1,1,24,768]{7,6,0,5,4,3,2,1:T(8,128)(2,1)S(1)} %constant_dynamic-slice_fusion.5), channel_id=1, source_target_pairs={{0,2},{1,3},{2,0},{3,1},{4,6},{5,7},{6,4},{7,5},{8,10},{9,11},{10,... | collective-permute-start | bytes 221192 | tf_op jit(solution)/shard_map/ppermute | solution.py:683
  432.3 4.4 collective-permute-start.39
  433.5 4.4 collective-permute-start.44
  439.2 10.9 %collective-permute-start.57 = (bf16[2,2,1,1,1,64,768]{6,5,4,3,2,1,0:T(8,128)(2,1)S(1)}, bf16[2,2,1,1,1,64,768]{6,5,4,3,2,1,0:T(8,128)(2,1)S(1)}, u32[]{:S(2)}, u32[]{:S(2)}) collective-permute-start(bf16[2,2,1,1,1,64,768]{6,5,4,3,2,1,0:T(8,128)(2,1)S(1)} %constant_dynamic-slice_fusion.2), channel_id=1, source_target_pairs={{0,4},{4,0},{8,12},{12,8},{16,20},{20,16},{24,28},{28,24},{1,5},{5... | collective-permute-start | bytes 1179656 | tf_op jit(solution)/shard_map/ppermute | solution.py:683
  450.5 10.9 %collective-permute-start.58 = (bf16[1,2,1,1,1,64,768]{6,5,4,3,2,1,0:T(8,128)(2,1)S(1)}, bf16[1,2,1,1,1,64,768]{6,5,4,3,2,1,0:T(8,128)(2,1)S(1)}, u32[]{:S(2)}, u32[]{:S(2)}) collective-permute-start(bf16[1,2,1,1,1,64,768]{6,5,4,3,2,1,0:T(8,128)(2,1)S(1)} %constant_dynamic-slice_fusion.1), channel_id=1, source_target_pairs={{0,16},{4,20},{8,24},{12,28},{16,0},{20,4},{24,8},{28,12},{1,17},{... | collective-permute-start | bytes 589832 | tf_op jit(solution)/shard_map/ppermute | solution.py:683
  461.5 4.7 collective-permute-start.59
  469.5 4.3 collective-permute-start.60
  475.1 6.3 %collective-permute-start.62 = (f32[107,128]{1,0:T(8,128)S(1)}, f32[107,128]{1,0:T(8,128)S(1)}, u32[]{:S(2)}, u32[]{:S(2)}) collective-permute-start(f32[107,128]{1,0:T(8,128)S(1)} %add.264), channel_id=1, source_target_pairs={{0,16},{4,20},{8,24},{12,28},{16,0},{20,4},{24,8},{28,12},{1,17},{... | collective-permute-start | bytes 164360 | tf_op jit(solution)/shard_map/ppermute | solution.py:683
  481.4 4.2 collective-permute-start.63
  485.7 4.2 collective-permute-start.64
  (31 other events, 172.8 us)
Sparse Core Ops, SparseCore 0:
  19.3 90.9 all-gather.1
  313.7 138.0 reduce-scatter.3
